TPU v7x, 32 devices: a whole 2x2x4 slice. The times are simulated.
32 devices in a mesh: rep: 8 (over y, x, core), shard: 4 (over z).
Axes of the slice: x: 2, y: 2, z: 4, core: 2. Of those that a mesh axis runs over, the one named last changes fastest.
Arguments:
- tokens: bfloat16 [8, 1024, 768], P('rep', 'shard'), may hold values from -6 to 6
- w_qkv: bfloat16 [3, 4, 192, 192], P(None, None, 'shard'), may hold values from -0.4375 to 0.4375
- b_qv: bfloat16 [2, 768], P(None, 'shard'), may hold values from -1.5 to 1.5
- w_attn: bfloat16 [768, 768], P('shard'), may hold values from -1.25 to 1.25
- b_attn: bfloat16 [768], P('shard'), may hold values from -1.5 to 1.5
- ln1_gain: bfloat16 [768], P('shard'), may hold values from 0.5 to 1.5
- ln1_bias: bfloat16 [768], P('shard'), may hold values from -1.5 to 1.5
- w_inter: bfloat16 [4, 192, 768], P(None, 'shard'), may hold values from -0.4375 to 0.4375
- b_inter: bfloat16 [3072], P('shard'), may hold values from -2.5 to 2.5
- w_output: bfloat16 [4, 768, 192], P(None, 'shard'), may hold values from -0.21875 to 0.21875
- b_output: bfloat16 [768], P('shard'), may hold values from -1.5 to 1.5
- ln2_gain: bfloat16 [768], P('shard'), may hold values from 0.5 to 1.5
- ln2_bias: bfloat16 [768], P('shard'), may hold values from -1.5 to 1.5
- segment_ids: int32 [8, 1024], P('rep'), may hold values from 0 to 6, as said below
- keep_mask: int32 [8, 1024], P('rep'), may hold values 0 or 1
- cotangent: bfloat16 [8, 1024, 768], P('rep', 'shard'), may hold values from -6 to 6
Outputs:
- output: bfloat16 [8, 1024, 768], P('rep', 'shard')
- d_tokens: float32 [8, 1024, 768], P('rep', 'shard')
- g_w_qkv: float32 [3, 4, 192, 192], P(None, None, 'shard')
- g_b_qv: float32 [2, 768], P(None, 'shard')
- g_w_attn: float32 [768, 768], P('shard')
- g_b_attn: float32 [768], P('shard')
- g_ln1_gain: float32 [768], P('shard')
- g_ln1_bias: float32 [768], P('shard')
- g_w_inter: float32 [4, 192, 768], P(None, 'shard')
- g_b_inter: float32 [3072], P('shard')
- g_w_output: float32 [4, 768, 192], P(None, 'shard')
- g_b_output: float32 [768], P('shard')
- g_ln2_gain: float32 [768], P('shard')
- g_ln2_bias: float32 [768], P('shard')
Inputs may be any that keep to these rules, and one draw needn't show every extreme that they name: `segment_ids`: along each sequence the document numbers never fall and each number covers at least one position.
All inputs are finite; a program needn't handle non-finite values. No bound on the sum of `keep_mask` on one device may be relied on, other than what follows from the above.
Results may differ from a plain program's by a relative error of at most 0.012.
Values may be sent and summed in bfloat16 or wider, within the bound.
No kernel may reach another device: no remote copies, remote signals or barrier semaphores. Data moves between devices by JAX's collectives and lax.ppermute only.
A program may use at most 128 MiB of HBM per device.

v0:
```python
from functools import partial
import math

import jax
import jax.numpy as jnp
from jax import lax
from jax.sharding import PartitionSpec as P

HEADS = 12
HEAD = 64
GROUPS = 4


epsilon = 1e-05
masked_score = -1e30


def layer_norm(residual, gain_vec, shift_vec):
    centre = residual - jnp.mean(residual, axis=-1, keepdims=True)
    spread = jnp.mean(centre * centre, axis=-1, keepdims=True)
    return centre * lax.rsqrt(spread + epsilon) * gain_vec + shift_vec


def heads_split(tensor, head_pairs):
    lead_dim, row_count = (tensor.shape[0], tensor.shape[1])
    shaped = tensor.reshape(lead_dim, row_count, head_pairs, 2, HEAD).transpose(0, 2, 3, 1, 4)
    return shaped.reshape(lead_dim * head_pairs, 2, row_count, HEAD)


def heads_merge(tensor, lead_dim):
    block_count, row_count = (tensor.shape[0], tensor.shape[2])
    head_pairs = block_count // lead_dim
    shaped = tensor.reshape(lead_dim, head_pairs, 2, row_count, HEAD).transpose(0, 3, 1, 2, 4)
    return shaped.reshape(lead_dim, row_count, head_pairs * 2 * HEAD)


def split_blocks(tensor, width):
    return tensor.reshape(tensor.shape[0], -1, width, tensor.shape[-1]).transpose(1, 0, 2, 3)


def merge_blocks(tensor):
    return tensor.transpose(1, 0, 2, 3).reshape(tensor.shape[1], -1, tensor.shape[-1])


def allowed_mask(seg_rows, seg_cols, keep_cols, row_offset, col_offset):
    row_count = seg_rows.shape[0]
    col_count = seg_cols.shape[0]
    row_places = row_offset + jnp.arange(row_count, dtype=jnp.int32)
    col_places = col_offset + jnp.arange(col_count, dtype=jnp.int32)
    same_doc = (seg_rows[:, None] == seg_cols[None, :]) & (keep_cols[None, :] == 1)
    return same_doc | (row_places[:, None] == col_places[None, :])


def masked_scores(
    query_blk, key_piece, seg_q, seg_piece, keep_piece, row_offset, col_offset, factor
):
    allowed = allowed_mask(seg_q, seg_piece, keep_piece, row_offset, col_offset)
    scores = (
        jnp.einsum("hqd,hkd->hqk", query_blk, key_piece, preferred_element_type=jnp.float32)
        * factor
    )
    return jnp.where(allowed[None], scores, masked_score)


def body(
    tokens,
    w_qkv,
    b_qv,
    w_attn,
    b_attn,
    ln1_gain,
    ln1_bias,
    w_inter,
    b_inter,
    w_output,
    b_output,
    ln2_gain,
    ln2_bias,
    segment_ids,
    keep_mask,
    cotangent,
):
    seq_count, tok_local, model_width = tokens.shape
    head_pairs = HEADS // 2
    factor = HEAD ** (-0.5)
    length = tok_local * lax.axis_size("shard")
    block_cols = math.gcd(length, 1024)
    offset = lax.axis_index("shard") * tok_local
    flat_rows = seq_count * tok_local
    seg_own = lax.dynamic_slice_in_dim(segment_ids, offset, tok_local, 1)
    rep_own = jnp.repeat(seg_own, head_pairs, axis=0)
    rep_all = jnp.repeat(segment_ids, head_pairs, axis=0)
    rep_keep = jnp.repeat(keep_mask, head_pairs, axis=0)
    block_starts = jnp.arange(length // block_cols, dtype=jnp.int32) * block_cols
    qkv_full, bias_qv, dense_w, dense_b, gain_one, shift_one = (
        lax.all_gather(w_qkv, "shard", axis=2, tiled=True),
        lax.all_gather(b_qv, "shard", axis=1, tiled=True),
        lax.all_gather(w_attn, "shard", axis=0, tiled=True),
        lax.all_gather(b_attn, "shard", axis=0, tiled=True),
        lax.all_gather(ln1_gain, "shard", axis=0, tiled=True),
        lax.all_gather(ln1_bias, "shard", axis=0, tiled=True),
    )
    grouped = tokens.reshape(flat_rows, GROUPS, model_width // GROUPS)
    qkv_mixed = jnp.einsum(
        "rgc,kgcd->krgd", grouped, qkv_full, preferred_element_type=jnp.float32
    ).reshape(3, seq_count, tok_local, model_width)
    queries = (qkv_mixed[0] + bias_qv[0].astype(jnp.float32)).astype(jnp.bfloat16)
    keys_own = qkv_mixed[1].astype(jnp.bfloat16)
    values_own = (qkv_mixed[2] + bias_qv[1].astype(jnp.float32)).astype(jnp.bfloat16)
    keys_all, values_all = (
        lax.all_gather(keys_own, "shard", axis=1, tiled=True),
        lax.all_gather(values_own, "shard", axis=1, tiled=True),
    )
    queries_h = heads_split(queries, head_pairs)
    keys_h = heads_split(keys_all, head_pairs)
    values_h = heads_split(values_all, head_pairs)

    def forward_block(operands):
        query_blk, key_blk, value_blk, seg_q, seg_k, keep_k = operands
        keys_b = split_blocks(key_blk, block_cols)
        values_b = split_blocks(value_blk, block_cols)
        segs_b = seg_k.reshape(-1, block_cols)
        keeps_b = keep_k.reshape(-1, block_cols)
        row_shape = query_blk.shape[:2]

        def peak_step(carry, pieces):
            peak, total = carry
            key_piece, seg_piece, keep_piece, start = pieces
            masked = masked_scores(
                query_blk, key_piece, seg_q, seg_piece, keep_piece, offset, start, factor
            )
            new_peak = jnp.maximum(peak, jnp.max(masked, axis=-1))
            total = total * jnp.exp(peak - new_peak) + jnp.sum(
                jnp.exp(masked - new_peak[..., None]), axis=-1
            )
            return ((new_peak, total), None)

        (peak, total), _ = lax.scan(
            peak_step,
            (jnp.full(row_shape, masked_score, jnp.float32), jnp.zeros(row_shape, jnp.float32)),
            (keys_b, segs_b, keeps_b, block_starts),
        )
        logsum = peak + jnp.log(total)

        def value_step(acc, pieces):
            key_piece, value_piece, seg_piece, keep_piece, start = pieces
            masked = masked_scores(
                query_blk, key_piece, seg_q, seg_piece, keep_piece, offset, start, factor
            )
            prob_low = jnp.exp(masked - logsum[..., None]).astype(jnp.bfloat16)
            return (
                acc
                + jnp.einsum(
                    "hqk,hkd->hqd", prob_low, value_piece, preferred_element_type=jnp.float32
                ),
                None,
            )

        attended_blk, _ = lax.scan(
            value_step,
            jnp.zeros(query_blk.shape, jnp.float32),
            (keys_b, values_b, segs_b, keeps_b, block_starts),
        )
        return (attended_blk, logsum)

    attended_h, logsums = lax.map(
        forward_block, (queries_h, keys_h, values_h, rep_own, rep_all, rep_keep)
    )
    attended = (
        heads_merge(attended_h, seq_count).astype(jnp.bfloat16).reshape(flat_rows, model_width)
    )
    projected = jnp.dot(attended, dense_w, preferred_element_type=jnp.float32)
    resid_one = (
        tokens.reshape(flat_rows, model_width).astype(jnp.float32)
        + projected
        + dense_b.astype(jnp.float32)
    )
    first_norm, norm_one_pull = jax.vjp(
        layer_norm, resid_one, gain_one.astype(jnp.float32), shift_one.astype(jnp.float32)
    )
    first_low = first_norm.astype(jnp.bfloat16).reshape(flat_rows, GROUPS, model_width // GROUPS)
    inter_w, inter_b, out_w, out_b, gain_two, shift_two = (
        lax.all_gather(w_inter, "shard", axis=1, tiled=True),
        lax.all_gather(b_inter, "shard", axis=0, tiled=True),
        lax.all_gather(w_output, "shard", axis=1, tiled=True),
        lax.all_gather(b_output, "shard", axis=0, tiled=True),
        lax.all_gather(ln2_gain, "shard", axis=0, tiled=True),
        lax.all_gather(ln2_bias, "shard", axis=0, tiled=True),
    )
    hidden = jnp.einsum(
        "rgc,gcf->rgf", first_low, inter_w, preferred_element_type=jnp.float32
    ) + inter_b.astype(jnp.float32).reshape(GROUPS, -1)
    activated, gelu_pull = jax.vjp(partial(jax.nn.gelu, approximate=False), hidden)
    activated_low = activated.astype(jnp.bfloat16)
    outward = jnp.einsum(
        "rgf,gfd->rgd", activated_low, out_w, preferred_element_type=jnp.float32
    ).reshape(flat_rows, model_width) + out_b.astype(jnp.float32)
    normed, norm_two_pull = jax.vjp(
        layer_norm,
        first_norm + outward,
        gain_two.astype(jnp.float32),
        shift_two.astype(jnp.float32),
    )
    output = normed.astype(jnp.bfloat16).reshape(seq_count, tok_local, model_width)
    grad_out = cotangent.reshape(flat_rows, model_width).astype(jnp.float32)
    d_resid_two, d_gain_two, d_shift_two = norm_two_pull(grad_out)
    d_out_b = jnp.sum(d_resid_two, axis=0)
    d_out_low = d_resid_two.astype(jnp.bfloat16).reshape(flat_rows, GROUPS, -1)
    d_out_w = jnp.einsum(
        "rgf,rgd->gfd", activated_low, d_out_low, preferred_element_type=jnp.float32
    )
    d_activated = jnp.einsum("rgd,gfd->rgf", d_out_low, out_w, preferred_element_type=jnp.float32)
    (d_hidden,) = gelu_pull(d_activated)
    d_inter_b = jnp.sum(d_hidden, axis=0).reshape(-1)
    d_hidden_low = d_hidden.astype(jnp.bfloat16)
    d_inter_w = jnp.einsum(
        "rgc,rgf->gcf", first_low, d_hidden_low, preferred_element_type=jnp.float32
    )
    d_first = d_resid_two + jnp.einsum(
        "rgf,gcf->rgc", d_hidden_low, inter_w, preferred_element_type=jnp.float32
    ).reshape(flat_rows, model_width)
    d_resid_one, d_gain_one, d_shift_one = norm_one_pull(d_first)
    d_dense_b = jnp.sum(d_resid_one, axis=0)
    d_proj_low = d_resid_one.astype(jnp.bfloat16)
    d_dense_w = jnp.einsum("rc,rd->cd", attended, d_proj_low, preferred_element_type=jnp.float32)
    d_attended = (
        jnp.einsum("rd,cd->rc", d_proj_low, dense_w, preferred_element_type=jnp.float32)
        .astype(jnp.bfloat16)
        .reshape(seq_count, tok_local, model_width)
    )
    d_attended_h = heads_split(d_attended, head_pairs)

    def query_back(operands, with_keys):
        query_blk, key_blk, value_blk, grad_blk, logsum_blk, seg_q, seg_k, keep_k = operands
        keys_b = split_blocks(key_blk, block_cols)
        values_b = split_blocks(value_blk, block_cols)
        segs_b = seg_k.reshape(-1, block_cols)
        keeps_b = keep_k.reshape(-1, block_cols)
        pieces_all = (keys_b, values_b, segs_b, keeps_b, block_starts)

        def inner_step(acc, pieces):
            key_piece, value_piece, seg_piece, keep_piece, start = pieces
            masked = masked_scores(
                query_blk, key_piece, seg_q, seg_piece, keep_piece, offset, start, factor
            )
            prob_full = jnp.exp(masked - logsum_blk[..., None])
            d_probs = jnp.einsum(
                "hqd,hkd->hqk", grad_blk, value_piece, preferred_element_type=jnp.float32
            )
            return (acc + jnp.sum(prob_full * d_probs, axis=-1), None)

        inner_prod, _ = lax.scan(inner_step, jnp.zeros(logsum_blk.shape, jnp.float32), pieces_all)

        def grad_step(d_query, pieces):
            key_piece, value_piece, seg_piece, keep_piece, start = pieces
            masked = masked_scores(
                query_blk, key_piece, seg_q, seg_piece, keep_piece, offset, start, factor
            )
            prob_full = jnp.exp(masked - logsum_blk[..., None])
            d_probs = jnp.einsum(
                "hqd,hkd->hqk", grad_blk, value_piece, preferred_element_type=jnp.float32
            )
            d_scores = (prob_full * (d_probs - inner_prod[..., None])).astype(jnp.bfloat16)
            d_query = (
                d_query
                + jnp.einsum(
                    "hqk,hkd->hqd", d_scores, key_piece, preferred_element_type=jnp.float32
                )
                * factor
            )
            d_key = (
                jnp.einsum("hqk,hqd->hkd", d_scores, query_blk, preferred_element_type=jnp.float32)
                * factor
            )
            d_value = jnp.einsum(
                "hqk,hqd->hkd",
                prob_full.astype(jnp.bfloat16),
                grad_blk,
                preferred_element_type=jnp.float32,
            )
            return (d_query, (d_key, d_value))

        d_query, key_terms = lax.scan(
            grad_step, jnp.zeros(query_blk.shape, jnp.float32), pieces_all
        )
        return (d_query, merge_blocks(key_terms[0]), merge_blocks(key_terms[1]))

    d_query_h, d_key_h, d_value_h = lax.map(
        partial(query_back, with_keys=True),
        (queries_h, keys_h, values_h, d_attended_h, logsums, rep_own, rep_all, rep_keep),
    )
    d_keys_part = heads_merge(d_key_h, seq_count)
    d_values_part = heads_merge(d_value_h, seq_count)
    d_keys, d_values = (
        lax.psum_scatter(d_keys_part, "shard", scatter_dimension=1, tiled=True),
        lax.psum_scatter(d_values_part, "shard", scatter_dimension=1, tiled=True),
    )
    d_queries = heads_merge(d_query_h, seq_count)
    d_stack = (
        jnp.stack([d_queries, d_keys, d_values])
        .astype(jnp.bfloat16)
        .reshape(3, flat_rows, GROUPS, model_width // GROUPS)
    )
    d_qkv_w = jnp.einsum("rgc,krgd->kgcd", grouped, d_stack, preferred_element_type=jnp.float32)
    d_bias_qv = jnp.stack(
        [
            jnp.sum(d_stack[0].astype(jnp.float32), axis=0).reshape(-1),
            jnp.sum(d_stack[2].astype(jnp.float32), axis=0).reshape(-1),
        ]
    )
    d_tokens = d_resid_one + jnp.einsum(
        "krgd,kgcd->rgc", d_stack, qkv_full, preferred_element_type=jnp.float32
    ).reshape(flat_rows, model_width)
    (
        g_qkv,
        g_bqv,
        g_dense,
        g_dense_b,
        g_gain_one,
        g_shift_one,
        g_inter,
        g_inter_b,
        g_out,
        g_out_b,
        g_gain_two,
        g_shift_two,
    ) = (
        lax.psum_scatter(d_qkv_w, "shard", scatter_dimension=2, tiled=True),
        lax.psum_scatter(d_bias_qv, "shard", scatter_dimension=1, tiled=True),
        lax.psum_scatter(d_dense_w, "shard", scatter_dimension=0, tiled=True),
        lax.psum_scatter(d_dense_b, "shard", scatter_dimension=0, tiled=True),
        lax.psum_scatter(d_gain_one, "shard", scatter_dimension=0, tiled=True),
        lax.psum_scatter(d_shift_one, "shard", scatter_dimension=0, tiled=True),
        lax.psum_scatter(d_inter_w, "shard", scatter_dimension=1, tiled=True),
        lax.psum_scatter(d_inter_b, "shard", scatter_dimension=0, tiled=True),
        lax.psum_scatter(d_out_w, "shard", scatter_dimension=1, tiled=True),
        lax.psum_scatter(d_out_b, "shard", scatter_dimension=0, tiled=True),
        lax.psum_scatter(d_gain_two, "shard", scatter_dimension=0, tiled=True),
        lax.psum_scatter(d_shift_two, "shard", scatter_dimension=0, tiled=True),
    )
    summed = lax.psum(
        (
            g_qkv,
            g_bqv,
            g_dense,
            g_dense_b,
            g_gain_one,
            g_shift_one,
            g_inter,
            g_inter_b,
            g_out,
            g_out_b,
            g_gain_two,
            g_shift_two,
        ),
        "rep",
    )
    return (
        output,
        d_tokens.reshape(seq_count, tok_local, model_width),
        summed[0],
        summed[1],
        summed[2],
        summed[3],
        summed[4],
        summed[5],
        summed[6],
        summed[7],
        summed[8],
        summed[9],
        summed[10],
        summed[11],
    )


def solution(mesh):
    in_specs = (
        P("rep", "shard", None),
        P(None, None, "shard", None),
        P(None, "shard"),
        P("shard", None),
        P("shard"),
        P("shard"),
        P("shard"),
        P(None, "shard", None),
        P("shard"),
        P(None, "shard", None),
        P("shard"),
        P("shard"),
        P("shard"),
        P("rep", None),
        P("rep", None),
        P("rep", "shard", None),
    )
    out_specs = (
        P("rep", "shard", None),
        P("rep", "shard", None),
        P(None, None, "shard", None),
        P(None, "shard"),
        P("shard", None),
        P("shard"),
        P("shard"),
        P("shard"),
        P(None, "shard", None),
        P("shard"),
        P(None, "shard", None),
        P("shard"),
        P("shard"),
        P("shard"),
    )
    return jax.shard_map(body, mesh=mesh, in_specs=in_specs, out_specs=out_specs, check_vma=False)
```

profile of v0, /device:TPU:0, one launch (start us, length us, event | category | flops | bytes accessed | tf_op | source)
XLA Modules:
  0.0 792.8 jit_solution(13025910028456460920)
XLA Ops:
  8.2 25.6 %all_gather.42 = bf16[3,4,192,192]{3,2,0,1:T(8,128)(2,1)S(1)} all-gather(bf16[3,4,48,192]{3,2,0,1:T(8,128)(2,1)S(1)} %copy.58), channel_id=1, replica_groups=mesh['rep'=8,'shard'=4] {'shard'}, dimensions={2}, use_global_device_ids=true | all-gather | bytes 1105920 | tf_op jit(solution)/shard_map/all_gather | solution.py:96
  33.9 2.2 copy.59
  36.1 1.6 convolution_bitcast_fusion.3
  38.6 10.8 %all-gather = bf16[4,192,2]{1,2,0:T(2,128)(2,1)S(1)} all-gather(bf16[1,192,2]{1,2,0:T(2,128)(2,1)S(1)} %bitcast.362), channel_id=1, replica_groups=mesh['rep'=8,'shard'=4] {'shard'}, dimensions={0}, use_global_device_ids=true | all-gather | bytes 3840 | tf_op jit(solution)/shard_map/all_gather | solution.py:97
  52.9 2.0 copy.62
  55.1 13.2 %all-gather.1 = bf16[4,1,768]{2,1,0:T(2,128)(2,1)S(1)} all-gather(bf16[1,1,768]{2,1,0:T(2,128)(2,1)S(1)} %reshape.617), channel_id=1, replica_groups=mesh['rep'=8,'shard'=4] {'shard'}, dimensions={0}, use_global_device_ids=true | all-gather | bytes 7680 | tf_op jit(solution)/shard_map/all_gather | solution.py:184
  71.6 16.3 %all-reduce.17 = (bf16[768]{0:T(1024)(128)(2,1)S(1)}, bf16[768]{0:T(1024)(128)(2,1)S(1)}, bf16[768]{0:T(1024)(128)(2,1)S(1)}, bf16[768]{0:T(1024)(128)(2,1)S(1)}...) all-reduce(bf16[768]{0:T(1024)(128)(2,1)S(1)} %dynamic-update-slice, ...), channel_id=1, replica_groups=mesh['rep'=8,'shard'=4] {'shard'}, use_global_device_ids=true, to_apply=%add | all-reduce | flops 4608 | bytes 18432
  90.0 26.1 %all-gather.10.cloned.1.call-done = bf16[1,1024,768]{1,2,0:T(8,128)(2,1)} async-done(((bf16[1,256,768]{1,2,0:T(8,128)(2,1)}), bf16[1,1024,768]{1,2,0:T(8,128)(2,1)}) %all-gather.10.cloned.1.call-update) | async-done | bytes 1572880 | tf_op jit(solution)/shard_map/all_gather | solution.py:112
  116.2 28.3 %while.24 = (s32[]{:T(128)}, bf16[6,2,256,64]{2,3,1,0:T(8,128)(2,1)S(1)}, f32[6,2,256]{2,1,0:T(2,128)}, s32[6,256]{1,0:T(8,128)S(1)}, s32[6,1024]{1,0:T(8,128)S(...) while((s32[]{:T(128)}, ...), condition=%wide.region_3.4_spmd, body=%wide.region_0.3_spmd.sunk | while | flops 138942208 | bytes 7586953 | solution.py:166
  116.6 1.6 fusion.139
  118.8 1.5 fusion.140
  121.3 1.6 fusion.139
  123.5 1.5 fusion.140
  126.1 1.6 fusion.139
  128.2 1.5 fusion.140
  130.8 1.6 fusion.139
  132.9 1.5 fusion.140
  135.5 1.6 fusion.139
  137.6 1.5 fusion.140
  140.2 1.6 fusion.139
  142.3 1.5 fusion.140
  144.5 1.9 all-gather.12.cloned.1.call-done
  146.4 1.9 fusion.96
  148.9 28.5 %all-gather.14.cloned.1.call-done = bf16[4,192,768]{2,1,0:T(8,128)(2,1)} async-done(((bf16[4,48,768]{2,1,0:T(8,128)(2,1)}), bf16[4,192,768]{2,1,0:T(8,128)(2,1)}) %all-gather.14.cloned.1.call-update) | async-done | bytes 1179664 | tf_op jit(solution)/shard_map/all_gather | solution.py:183
  177.4 10.0 %fusion.51 = (bf16[256,4,768]{2,0,1:T(8,128)(2,1)S(1)}, f32[256,4,768]{2,0,1:T(8,128)}, f32[4,256,768]{2,1,0:T(8,128)}) fusion(f32[4,768]{1,0:T(4,128)} %bitcast.357, bf16[256,4,192]{0,2,1:T(8,128)(2,1)S(1)} %bitcast.336, bf16[4,192,768]{2,1,0:T(8,128)(2,1)} %all-gather.14.cloned.1.call-done), kind=kOutput, calls=%fused_computation.85 | convolution fusion | flops 353894400 | bytes 9449472 | tf_op jit(solution)/shard_map/rgc,gcf->rgf/dot_general | solution.py:190
  187.4 28.2 %all-gather.16.cloned.1.call-done = bf16[4,768,192]{2,0,1:T(4,128)(2,1)} async-done(((bf16[4,192,192]{2,0,1:T(4,128)(2,1)}), bf16[4,768,192]{2,0,1:T(4,128)(2,1)}) %all-gather.16.cloned.1.call-update) | async-done | bytes 1179664 | tf_op jit(solution)/shard_map/all_gather | solution.py:185
  215.6 3.0 fusion.64
  218.6 2.3 copy.64
  221.0 1.5 fusion.91
  226.5 6.0 fusion.97
  232.5 1.5 fusion.76
  234.0 2.3 copy.67
  236.3 2.3 multiply_reduce_fusion.1
  241.0 59.1 %while.25 = (s32[]{:T(128)}, bf16[6,2,256,64]{2,3,1,0:T(8,128)(2,1)S(1)}, f32[6,2,1024,64]{2,3,1,0:T(8,128)}, f32[6,2,1024,64]{2,3,1,0:T(8,128)}, s32[6,256]{1,0...) while((s32[]{:T(128)}, ...), condition=%wide.region_14.15_spmd, body=%wide.region_12.14_spmd.sunk | while | flops 341476096 | bytes 18520224 | solution.py:288
  241.1 1.4 fusion.149
  245.1 2.0 multiply_reduce_fusion.6
  250.9 1.4 fusion.149
  254.9 2.0 multiply_reduce_fusion.6
  264.8 2.0 multiply_reduce_fusion.6
  270.6 1.4 fusion.149
  274.6 2.0 multiply_reduce_fusion.6
  284.5 2.0 multiply_reduce_fusion.6
  290.3 1.4 fusion.149
  294.4 2.0 multiply_reduce_fusion.6
  301.0 58.5 %reduce-scatter.11.cloned.1.call-done = f32[1,256,768]{1,2,0:T(8,128)} async-done(((f32[1,1024,768]{1,2,0:T(8,128)}), f32[1,256,768]{1,2,0:T(8,128)}) %reduce-scatter.11.cloned.1.call-update) | async-done | bytes 786448 | tf_op jit(solution)/shard_map/reduce_scatter | solution.py:296
  360.8 61.3 %reduce-scatter.9.cloned.1.call-done = f32[1,256,768]{1,2,0:T(8,128)} async-done(((f32[1,1024,768]{1,2,0:T(8,128)}), f32[1,256,768]{1,2,0:T(8,128)}) %reduce-scatter.9.cloned.1.call-update) | async-done | bytes 786448 | tf_op jit(solution)/shard_map/reduce_scatter | solution.py:295
  424.0 1.9 convolution_bitcast_fusion.2
  425.9 4.5 copy.70
  430.5 2.0 fusion.88
  432.6 1.9 fusion.74
  436.0 2.4 fusion.98
  440.5 85.7 %all-reduce.21.cloned.1.call-done = f32[3,4,192,192]{3,1,0,2:T(4,128)} async-done(((f32[3,4,192,192]{3,1,0,2:T(4,128)}), f32[3,4,192,192]{3,1,0,2:T(4,128)}) %all-reduce.21.cloned.1.call-update) | async-done | bytes 1769488
  526.3 1.9 constant_dynamic-slice_fusion.5
  528.2 47.5 %reduce-scatter.13.cloned.1.call-done = f32[192,768]{1,0:T(8,128)} async-done(((f32[768,768]{1,0:T(8,128)}), f32[192,768]{1,0:T(8,128)}) %reduce-scatter.13.cloned.1.call-update) | async-done | bytes 589840 | tf_op jit(solution)/shard_map/reduce_scatter | solution.py:330
  575.7 49.7 %reduce-scatter.15.cloned.1.call-done = f32[4,48,768]{2,1,0:T(8,128)} async-done(((f32[4,192,768]{2,1,0:T(8,128)}), f32[4,48,768]{2,1,0:T(8,128)}) %reduce-scatter.15.cloned.1.call-update) | async-done | bytes 589840 | tf_op jit(solution)/shard_map/reduce_scatter | solution.py:334
  625.4 62.1 %reduce-scatter.17.cloned.1.call-done = f32[4,192,192]{2,1,0:T(8,128)} async-done(((f32[4,768,192]{2,1,0:T(8,128)}), f32[4,192,192]{2,1,0:T(8,128)}) %reduce-scatter.17.cloned.1.call-update) | async-done | bytes 589840 | tf_op jit(solution)/shard_map/reduce_scatter | solution.py:336
  689.5 1.6 fusion.79
  691.5 1.7 add_reduce_fusion
  693.2 18.9 %all-reduce.16 = (f32[768]{0:T(1024)S(1)}, f32[768]{0:T(1024)S(1)}, f32[768]{0:T(1024)S(1)}, f32[3072]{0:T(1024)S(1)}, f32[768]{0:T(1024)S(1)}, /*index=5*/f32[768]{0:T(1024)S(1)}, f32[768]{0:T(1024)S(1)}) all-reduce(f32[768]{0:T(1024)S(1)} %get-tuple-element.413, ...), channel_id=7, replica_groups=mesh['rep'=8,'shard'=4] {'shard'}, use_global_device_ids=true, to_apply=%region_26.27.clone | all-reduce | flops 7680 | bytes 61440
  713.6 22.7 %all-reduce.14 = (f32[2,192]{1,0:T(2,128)}, f32[192]{0:T(256)}, f32[192]{0:T(256)}, f32[192]{0:T(256)}, f32[768]{0:T(1024)}, /*index=5*/f32[192]{0:T(256)}, f32[192]{0:T(256)}, f32[192]{0:T(256)}) all-reduce(f32[2,192]{1,0:T(2,128)S(1)} %copy.77, f32[192]{0:T(256)S(1)} %dynamic-slice.9, ...), channel_id=1, replica_groups=mesh['rep'=8,'shard'=4] {'rep'}, use_global_device_ids=true, to_apply=%region_22.23 | all-reduce | flops 2304 | bytes 18432 | tf_op jit(solution)/shard_map/psum | solution.py:341
  736.3 43.2 %all-reduce.23.cloned.1.call-done = (f32[3,4,48,192]{3,1,0,2:T(4,128)}, f32[192,768]{1,0:T(8,128)}, f32[4,48,768]{2,1,0:T(8,128)}, f32[4,192,192]{2,1,0:T(8,128)}) async-done(((f32[3,4,48,192]{3,1,0,2:T(4,128)}, f32[192,768]{1,0:T(8,128)}, f32[4,48,768]{2,1,0:T(8,128)}, f32[4,192,192]{2,1,0:T(8,128)}), (f32[3,4,48,192]{3,1,0,2:T(4,128)}, f32[192,768]{1,0:T(8,128)}, f32[4,48,768]{2,1,0:T(8,128)}, ...) | async-done | bytes 2211856 | tf_op jit(solution)/shard_map/psum | solution.py:341
  779.5 2.1 copy.72
  781.6 1.9 copy.126
  783.5 1.9 copy.127
  (321 shorter events, 78.4 us)
Async XLA Ops:
  7.2 82.8 %all-gather.8.cloned.1.call-start = ((), (), s32[]{:S(2)}) async-start(), calls=%async_computation.6 | async-start | bytes 1966080 | tf_op jit(solution)/shard_map/all_gather | solution.py:111
  33.9 16.7 %copy-start.3 = (bf16[3,4,192,192]{3,2,0,1:T(8,128)(2,1)}, bf16[3,4,192,192]{3,2,0,1:T(8,128)(2,1)S(1)}, u32[]{:S(2)}) copy-start(bf16[3,4,192,192]{3,2,0,1:T(8,128)(2,1)S(1)} %all_gather.42) | copy-start | bytes 2654212
  33.9 4.7 copy-start.43
  38.5 77.6 %all-gather.10.cloned.1.call-start = ((), (), s32[]{:S(2)}) async-start(), calls=%async_computation.7 | async-start | bytes 1966080 | tf_op jit(solution)/shard_map/all_gather | solution.py:112
  49.5 5.6 copy-start.42
  49.5 19.4 %copy-start.41 = (u32[32]{0:T(128)S(1)}, u32[32]{0:T(128)}, u32[]{:S(2)}) copy-start(u32[32]{0:T(128)} %constant.222) | copy-start | bytes 388
  49.5 40.2 %copy-start.39 = (s32[1,1024]{1,0:T(1,128)S(1)}, s32[1,1024]{1,0:T(1,128)}, u32[]{:S(2)}) copy-start(s32[1,1024]{1,0:T(1,128)} %param.33) | copy-start | bytes 12292
  50.6 19.6 %copy-start.44 = (bf16[192]{0:T(256)(128)(2,1)S(1)}, bf16[192]{0:T(256)(128)(2,1)}, u32[]{:S(2)}) copy-start(bf16[192]{0:T(256)(128)(2,1)} %param.24) | copy-start | bytes 1156
  50.6 19.9 %copy-start.45 = (bf16[192]{0:T(256)(128)(2,1)S(1)}, bf16[192]{0:T(256)(128)(2,1)}, u32[]{:S(2)}) copy-start(bf16[192]{0:T(256)(128)(2,1)} %param.26) | copy-start | bytes 1156
  50.6 20.1 %copy-start.46 = (bf16[192]{0:T(256)(128)(2,1)S(1)}, bf16[192]{0:T(256)(128)(2,1)}, u32[]{:S(2)}) copy-start(bf16[192]{0:T(256)(128)(2,1)} %param.25) | copy-start | bytes 1156
  50.6 20.3 %copy-start.47 = (bf16[192]{0:T(256)(128)(2,1)S(1)}, bf16[192]{0:T(256)(128)(2,1)}, u32[]{:S(2)}) copy-start(bf16[192]{0:T(256)(128)(2,1)} %param.30) | copy-start | bytes 1156
  50.6 20.5 %copy-start.48 = (bf16[192]{0:T(256)(128)(2,1)S(1)}, bf16[192]{0:T(256)(128)(2,1)}, u32[]{:S(2)}) copy-start(bf16[192]{0:T(256)(128)(2,1)} %param.32) | copy-start | bytes 1156
  50.6 20.8 %copy-start.49 = (bf16[192]{0:T(256)(128)(2,1)S(1)}, bf16[192]{0:T(256)(128)(2,1)}, u32[]{:S(2)}) copy-start(bf16[192]{0:T(256)(128)(2,1)} %param.31) | copy-start | bytes 1156
  50.6 39.1 %copy-start.9 = (f32[1,256,4,192]{1,3,0,2:T(8,128)S(1)}, f32[1,256,4,192]{1,3,0,2:T(8,128)}, u32[]{:S(2)}) copy-start(f32[1,256,4,192]{1,3,0,2:T(8,128)} %get-tuple-element.409) | copy-start | bytes 2359300
  50.6 65.5 %copy-start.40 = (s32[1,1024]{1,0:T(1,128)S(1)}, s32[1,1024]{1,0:T(1,128)}, u32[]{:S(2)}) copy-start(s32[1,1024]{1,0:T(1,128)} %param.34) | copy-start | bytes 12292
  51.6 94.8 %all-gather.12.cloned.1.call-start = ((), (), s32[]{:S(2)}) async-start(), calls=%async_computation.8 | async-start | bytes 1474560 | tf_op jit(solution)/shard_map/all_gather | solution.py:98
  52.3 125.1 %all-gather.14.cloned.1.call-start = ((), (), s32[]{:S(2)}) async-start(), calls=%async_computation.9 | async-start | bytes 1474560 | tf_op jit(solution)/shard_map/all_gather | solution.py:183
  52.9 162.7 %all-gather.16.cloned.1.call-start = ((), (), s32[]{:S(2)}) async-start(), calls=%async_computation.10 | async-start | bytes 1966080 | tf_op jit(solution)/shard_map/all_gather | solution.py:185
  55.0 304.5 %reduce-scatter.11.cloned.1.call-start = ((), (), s32[]{:S(2)}) async-start(), calls=%async_computation.12 | async-start | bytes 3932160 | tf_op jit(solution)/shard_map/reduce_scatter | solution.py:296
  88.0 60.6 %copy-start.24 = (f32[768]{0:T(1024)}, f32[768]{0:T(1024)S(1)}, u32[]{:S(2)}) copy-start(f32[768]{0:T(1024)S(1)} %convert_element_type.167) | copy-start | bytes 9220
  116.2 30.2 %copy-start.10 = (bf16[1,256,768]{2,1,0:T(8,128)(2,1)S(1)}, bf16[1,256,768]{2,1,0:T(8,128)(2,1)}, u32[]{:S(2)}) copy-start(bf16[1,256,768]{2,1,0:T(8,128)(2,1)} %param.20) | copy-start | bytes 1179652
  144.4 1.9 copy-start.21
  144.4 1.9 copy-start.22
  144.4 33.0 %copy-start.7 = (bf16[6,2,256,64]{2,3,1,0:T(8,128)(2,1)}, bf16[6,2,256,64]{2,3,1,0:T(8,128)(2,1)S(1)}, u32[]{:S(2)}) copy-start(bf16[6,2,256,64]{2,3,1,0:T(8,128)(2,1)S(1)} %get-tuple-element.268) | copy-start | bytes 1179652
  148.5 28.9 %copy-start.37 = (f32[256]{0:T(256)}, f32[256]{0:T(256)S(1)}, u32[]{:S(2)}) copy-start(f32[256]{0:T(256)S(1)} %multiply_reduce_fusion.4) | copy-start | bytes 3076
  148.5 28.9 %copy-start.26 = (f32[256]{0:T(256)}, f32[256]{0:T(256)S(1)}, u32[]{:S(2)}) copy-start(f32[256]{0:T(256)S(1)} %fusion.84) | copy-start | bytes 3076
  148.9 38.5 %copy-start.11 = (bf16[256,768]{0,1:T(8,128)(2,1)}, bf16[256,768]{0,1:T(8,128)(2,1)S(1)}, u32[]{:S(2)}) copy-start(bf16[256,768]{0,1:T(8,128)(2,1)S(1)} %copy.61) | copy-start | bytes 1179652
  187.4 35.0 %copy-start = (bf16[256,4,768]{2,0,1:T(8,128)(2,1)}, bf16[256,4,768]{2,0,1:T(8,128)(2,1)S(1)}, u32[]{:S(2)}) copy-start(bf16[256,4,768]{2,0,1:T(8,128)(2,1)S(1)} %get-tuple-element.402) | copy-start | bytes 4718596
  187.4 33.5 %copy-start.25 = (f32[768]{0:T(1024)S(1)}, f32[768]{0:T(1024)}, u32[]{:S(2)}) copy-start(f32[768]{0:T(1024)} %copy-done.24) | copy-start | bytes 9220
  187.4 33.5 %copy-start.27 = (f32[256]{0:T(256)S(1)}, f32[256]{0:T(256)}, u32[]{:S(2)}) copy-start(f32[256]{0:T(256)} %copy-done.26) | copy-start | bytes 3076
  187.4 33.5 %copy-start.34 = (f32[768]{0:T(1024)S(1)}, f32[768]{0:T(1024)}, u32[]{:S(2)}) copy-start(f32[768]{0:T(1024)} %convert_element_type.170) | copy-start | bytes 9220
  218.6 4.1 copy-start.5
  218.6 4.1 copy-start.23
  218.6 5.1 copy-start.33
  224.8 1.7 copy-start.38
  226.4 6.0 copy-start.17
  236.3 4.0 copy-start.2
  240.3 190.2 %copy-start.35 = (f32[256]{0:T(256)}, f32[256]{0:T(256)S(1)}, u32[]{:S(2)}) copy-start(f32[256]{0:T(256)S(1)} %negate_multiply_fusion.1) | copy-start | bytes 3076
  300.2 123.1 %copy-start.14 = (bf16[6,2,256,64]{2,3,1,0:T(8,128)(2,1)}, bf16[6,2,256,64]{2,3,1,0:T(8,128)(2,1)S(1)}, u32[]{:S(2)}) copy-start(bf16[6,2,256,64]{2,3,1,0:T(8,128)(2,1)S(1)} %get-tuple-element.270) | copy-start | bytes 1179652
  300.2 123.8 %copy-start.16 = (bf16[1,256,768]{1,2,0:T(8,128)(2,1)S(1)}, bf16[1,256,768]{1,2,0:T(8,128)(2,1)}, u32[]{:S(2)}) copy-start(bf16[1,256,768]{1,2,0:T(8,128)(2,1)} %copy.59) | copy-start | bytes 1179652
  300.2 121.9 %reduce-scatter.9.cloned.1.call-start = ((), (), s32[]{:S(2)}) async-start(), calls=%async_computation.11 | async-start | bytes 3932160 | tf_op jit(solution)/shard_map/reduce_scatter | solution.py:295
  301.0 225.3 %all-reduce.21.cloned.1.call-start = ((), (), s32[]{:S(2)}) async-start(), calls=%async_computation.17 | async-start | bytes 4718592
  360.8 69.6 %copy-start.19 = (bf16[1,256,768]{1,2,0:T(8,128)(2,1)}, bf16[1,256,768]{1,2,0:T(8,128)(2,1)S(1)}, u32[]{:S(2)}) copy-start(bf16[1,256,768]{1,2,0:T(8,128)(2,1)S(1)} %get-tuple-element.394) | copy-start | bytes 1179652
  423.3 0.7 copy-start.20
  425.9 4.6 copy-start.8
  430.4 2.2 copy-start.12
  430.5 145.2 %reduce-scatter.13.cloned.1.call-start = ((), (), s32[]{:S(2)}) async-start(), calls=%async_computation.13 | async-start | bytes 2949120 | tf_op jit(solution)/shard_map/reduce_scatter | solution.py:330
  432.6 2.1 copy-start.13
  432.6 192.8 %reduce-scatter.15.cloned.1.call-start = ((), (), s32[]{:S(2)}) async-start(), calls=%async_computation.14 | async-start | bytes 2949120 | tf_op jit(solution)/shard_map/reduce_scatter | solution.py:334
  434.5 1.4 copy-start.1
  434.6 4.6 copy-start.15
  434.6 252.9 %reduce-scatter.17.cloned.1.call-start = ((), (), s32[]{:S(2)}) async-start(), calls=%async_computation.15 | async-start | bytes 3932160 | tf_op jit(solution)/shard_map/reduce_scatter | solution.py:336
  438.4 250.4 %copy-start.6 = (bf16[1,256,768]{2,1,0:T(8,128)(2,1)S(1)}, bf16[1,256,768]{2,1,0:T(8,128)(2,1)}, u32[]{:S(2)}) copy-start(bf16[1,256,768]{2,1,0:T(8,128)(2,1)} %param.35) | copy-start | bytes 1179652
  438.4 251.1 %copy-start.36 = (f32[4,768]{1,0:T(4,128)S(1)}, f32[4,768]{1,0:T(4,128)}, u32[]{:S(2)}) copy-start(f32[4,768]{1,0:T(4,128)} %get-tuple-element.420) | copy-start | bytes 36868
  438.4 251.1 %copy-start.4 = (bf16[3,4,192,192]{3,2,0,1:T(8,128)(2,1)S(1)}, bf16[3,4,192,192]{3,2,0,1:T(8,128)(2,1)}, u32[]{:S(2)}) copy-start(bf16[3,4,192,192]{3,2,0,1:T(8,128)(2,1)} %copy-done.3) | copy-start | bytes 2654212
  438.4 274.2 %reduce-scatter.19.cloned.1.call-start = ((), (), s32[]{:S(2)}) async-start(), calls=%async_computation.16 | async-start | bytes 491520
  440.5 339.1 %all-reduce.23.cloned.1.call-start = ((), (), s32[]{:S(2)}) async-start(), calls=%async_computation.18 | async-start | bytes 5111808 | tf_op jit(solution)/shard_map/psum | solution.py:341
  689.5 3.7 copy-start.28
  691.2 2.0 copy-start.29
  691.2 2.0 copy-start.30
  691.2 2.0 copy-start.31
  691.2 2.0 copy-start.32
  779.5 5.9 copy-start.18
Sparse Core Ops, SparseCore 0:
  38.6 39.0 all-gather.7
  79.9 36.1 all-gather.9
  117.7 28.6 all-gather.11
  147.8 29.5 all-gather.13
  179.4 36.1 all-gather.15
  300.3 59.1 reduce-scatter.10
  361.8 60.2 reduce-scatter.8
  430.6 95.6 all-reduce.20
  528.6 47.0 reduce-scatter.12
  577.8 47.5 reduce-scatter.14
  627.7 59.7 reduce-scatter.16
  690.2 20.8 reduce-scatter.18
  715.8 63.7 all-reduce.22
where the time goes:
time: 796 us; the launch traced here: 793 us
  waiting for transfers between devices  495 us (62%)
  blocking collectives  108 us (14%)
  matrix products  94.9 us (12%)
  local copies, waits for them, and re-layouts  42.8 us (5%)
  other arithmetic  34.5 us (4%)
  between operations  17.3 us (2%)
    unnamed x15, waiting for transfers between devices  87.8 us
    reduce_scatter x1, waiting for transfers between devices, body(): lax.psum_scatter(d_out_w, 'shard', scatter_dimension=1, tiled=True)  62.1 us
    reduce_scatter x1, waiting for transfers between devices, body(): lax.psum_scatter(d_keys_part, 'shard', scatter_dimension=1, tiled=True)  61.3 us
    reduce_scatter x1, waiting for transfers between devices, body(): lax.psum_scatter(d_values_part, 'shard', scatter_dimension=1, tiled=True)  58.5 us
    reduce_scatter x1, waiting for transfers between devices, body(): lax.psum_scatter(d_inter_w, 'shard', scatter_dimension=1, tiled=True)  49.7 us
    reduce_scatter x1, waiting for transfers between devices, body(): lax.psum_scatter(d_dense_w, 'shard', scatter_dimension=0, tiled=True)  47.5 us
    psum x1, waiting for transfers between devices, body(): lax.psum((g_qkv, g_bqv, g_dense, g_dense_b, g_gain_one, g_shift_one, g_in...  43.2 us
    unnamed x2, blocking collectives  35.1 us
  transfers between devices with their start and end apart: 13, of which 11 were waited for; matrix products, arithmetic and copies ran while one was open for 8% of the time, Pallas kernels for 0%

commit v1 on v0

--- a/solution.py
+++ b/solution.py
@@ -4,6 +4,8 @@
 import jax
 import jax.numpy as jnp
 from jax import lax
+from jax.experimental import pallas as pl
+from jax.experimental.pallas import tpu as pltpu
 from jax.sharding import PartitionSpec as P
 
 HEADS = 12
@@ -373,6 +375,655 @@
     )
 
 
+BF = jnp.bfloat16
+F32 = jnp.float32
+I32 = jnp.int32
+VEC_ROWS = 16
+ROW_SPLIT = 4
+
+
+def mxu(a, b, dims):
+    return lax.dot_general(a, b, (dims, ((), ())), preferred_element_type=F32)
+
+
+def nn(a, b):
+    return mxu(a, b, ((1,), (0,)))
+
+
+def nt(a, b):
+    return mxu(a, b, ((1,), (1,)))
+
+
+def tn(a, b):
+    return mxu(a, b, ((0,), (0,)))
+
+
+def vmem(n):
+    return [pl.BlockSpec(memory_space=pltpu.VMEM)] * n
+
+
+def smem():
+    return pl.BlockSpec(memory_space=pltpu.SMEM)
+
+
+def call(kernel, outs, scratch=(), limit=None, name=None, cost=None):
+    def go(place, *args):
+        return pl.pallas_call(
+            kernel,
+            out_shape=outs,
+            in_specs=[smem()] + vmem(len(args)),
+            out_specs=tuple(vmem(len(outs))),
+            scratch_shapes=list(scratch),
+            compiler_params=pltpu.CompilerParams(vmem_limit_bytes=limit or (40 << 20)),
+            name=name,
+            cost_estimate=cost,
+        )(place, *args)
+
+    return go
+
+
+def aligned(index, size):
+    return pl.ds(pl.multiple_of(index * size, size), size)
+
+
+def packet_kernel(place, tokens, w_qkv, vectors, b_inter, *refs):
+    packets, turned = refs[:4], refs[4]
+    s = place[0]
+    rows, width = tokens.shape
+    part = width // 4
+    turned[...] = tokens[...].T
+    own = w_qkv.shape[2]
+    for d in range(4):
+        to = s ^ d
+        packets[d][0:part, :] = turned[aligned(to, part), :]
+        for t in range(3):
+            packets[d][part + t * own : part + (t + 1) * own, 0:part] = w_qkv[t, to]
+        packets[d][part + 3 * own :, :] = jnp.zeros((packets[d].shape[0] - part - 3 * own, rows), BF)
+    base = part + 3 * own
+    count = vectors.shape[0]
+    for shard in range(4):
+
+        @pl.when(s == shard)
+        def _():
+            spread = jnp.concatenate(
+                [jnp.zeros((count, part * shard), BF)] * (shard > 0)
+                + [vectors[...]]
+                + [jnp.zeros((count, part * (3 - shard)), BF)] * (shard < 3),
+                axis=1,
+            )
+            lines = jnp.concatenate(
+                [jnp.zeros((1, width), BF)] * shard + [b_inter[...]] + [jnp.zeros((1, width), BF)] * (3 - shard),
+                axis=0,
+            )
+            for piece in range(width // rows):
+                at = slice(rows * piece, rows * (piece + 1))
+                for d in range(4):
+                    top = base + VEC_ROWS * piece
+                    packets[d][top : top + count, :] = spread[:, at]
+                    packets[d][top + 8 : top + 12, :] = lines[:, at]
+
+
+def attention_kernel(place, p0, p1, p2, p3, bias_qv, segments, keep, *refs):
+    (o0, o1, o2, o3, weights, shares, inverse, q_all, k_all, v_all, w_all, k_rows, mask) = refs
+    packets, outs = (p0, p1, p2, p3), (o0, o1, o2, o3)
+    s = place[0]
+    head = pl.program_id(0)
+    block = o0.shape[1]
+    part = o0.shape[0]
+    own = part // 4
+    length = 4 * block
+
+    @pl.when(head == 0)
+    def _():
+        for d in range(4):
+            for t in range(3):
+                w_all[t, aligned(s ^ d, own), :] = packets[d][part + t * own : part + (t + 1) * own, 0:part]
+        for d in range(4):
+            cols = slice(block * d, block * (d + 1))
+            x = packets[d][0:part, :]
+            q = tn(w_all[0], x) + bias_qv[:, 0:1].astype(F32)
+            q_all[:, cols] = (q.astype(BF).astype(F32) * HEAD ** (-0.5)).astype(BF)
+            k_all[:, cols] = tn(w_all[1], x).astype(BF)
+            v_all[:, cols] = (tn(w_all[2], x) + bias_qv[:, 1:2].astype(F32)).astype(BF)
+        for h in range(part // HEAD):
+            k_rows[h] = k_all[HEAD * h : HEAD * (h + 1), :].T
+        seg_row = jnp.concatenate([segments[:, aligned(s ^ d, block)] for d in range(4)], axis=1)
+        for d in range(4):
+            code = jnp.where(keep[:, aligned(s ^ d, block)] == 1, segments[:, aligned(s ^ d, block)], -1)
+            column = jnp.broadcast_to(code.astype(F32), (128, block)).T
+            for c in range(4):
+                want = jnp.broadcast_to(seg_row[:, block * c : block * (c + 1)].astype(F32), (block, block))
+                same = jnp.concatenate([column] * (block // 128), axis=1) == want
+                if c == d:
+                    same = same | (
+                        lax.broadcasted_iota(I32, (block, block), 0) == lax.broadcasted_iota(I32, (block, block), 1)
+                    )
+                mask[block * d : block * (d + 1), block * c : block * (c + 1)] = jnp.where(same, 0.0, masked_score)
+
+    rows = aligned(head, HEAD)
+    for c in range(4):
+        cols = slice(block * c, block * (c + 1))
+        scores = nn(k_rows[head], q_all[rows, cols]) + mask[:, cols]
+        peak = jnp.max(scores, axis=0, keepdims=True)
+        terms = jnp.exp(scores - peak)
+        inv = 1.0 / jnp.sum(terms, axis=0, keepdims=True)
+        low = terms.astype(BF)
+        shares[0, :, cols] = low
+        inverse[head, :, cols] = inv
+        outs[c][rows, :] = (nn(v_all[rows, :], low) * inv).astype(BF)
+
+    @pl.when(head == 0)
+    def _():
+        weights[...] = w_all[...]
+
+
+def attention_forward(place, packets, bias_qv, segments, keep):
+    part = bias_qv.shape[0]
+    block = packets[0].shape[1]
+    length = 4 * block
+    heads = part // HEAD
+    whole = lambda shape: pl.BlockSpec(shape, lambda h: (0,) * len(shape))
+    sd = jax.ShapeDtypeStruct
+    outs = [sd((part, block), BF)] * 4 + [
+        sd((3, part, part), BF),
+        sd((heads, length, length), BF),
+        sd((heads, 1, length), F32),
+        sd((part, length), BF),
+        sd((part, length), BF),
+        sd((part, length), BF),
+    ]
+    out_specs = [whole(o.shape) for o in outs]
+    out_specs[5] = pl.BlockSpec((1, length, length), lambda h: (h, 0, 0))
+    args = (*packets, bias_qv, segments, keep)
+    return pl.pallas_call(
+        attention_kernel,
+        grid=(heads,),
+        out_shape=outs,
+        in_specs=[smem()] + [whole(a.shape) for a in args],
+        out_specs=out_specs,
+        scratch_shapes=[
+            pltpu.VMEM((3, part, part), BF),
+            pltpu.VMEM((heads, length, HEAD), BF),
+            pltpu.VMEM((length, length), F32),
+        ],
+        compiler_params=pltpu.CompilerParams(vmem_limit_bytes=48 << 20),
+        name="attention_forward",
+    )(place, *args)
+
+
+def attention_back_kernel(place, g0, g1, g2, g3, o0, o1, o2, o3, p0, p1, p2, p3, weights, shares, inverse, q_all, k_all, v_all, *refs):
+    (t0, t1, t2, t3, w0, w1, w2, w3, g_bias, d_q, d_k, d_v, marks) = refs
+    grads, outs, packets = (g0, g1, g2, g3), (o0, o1, o2, o3), (p0, p1, p2, p3)
+    s = place[0]
+    head = pl.program_id(0)
+    heads = pl.num_programs(0)
+    block = g0.shape[1]
+    part = g0.shape[0]
+    own = part // 4
+    rows = aligned(head, HEAD)
+    v_rows = v_all[rows, :].T
+    lows = []
+    for c in range(4):
+        cols = slice(block * c, block * (c + 1))
+        grad = grads[c][rows, :].astype(F32) * inverse[head, :, cols]
+        low = grad.astype(BF)
+        lows.append(low)
+        inner = jnp.sum(grad * outs[c][rows, :].astype(F32), axis=0, keepdims=True)
+        d_share = nn(v_rows, low)
+        marks[:, cols] = (shares[0, :, cols].astype(F32) * (d_share - inner)).astype(BF)
+        d_q[rows, cols] = (nn(k_all[rows, :], marks[:, cols]) * HEAD ** (-0.5)).astype(BF)
+    d_k[rows, :] = nt(q_all[rows, :], marks[...]).astype(BF)
+    d_v[rows, :] = nt(jnp.concatenate(lows, axis=1), shares[0]).astype(BF)
+
+    @pl.when(head == heads - 1)
+    def _():
+        x = jnp.concatenate([p[0:part, :] for p in packets], axis=1)
+        outgoing = (t0, t1, t2, t3)
+        for c in range(4):
+            cols = slice(block * c, block * (c + 1))
+            outgoing[c][...] = (
+                nn(weights[0], d_q[:, cols]) + nn(weights[1], d_k[:, cols]) + nn(weights[2], d_v[:, cols])
+            ).astype(BF)
+        totals = (w0, w1, w2, w3)
+        for t, d in enumerate((d_q, d_k, d_v)):
+            g = nt(x, d[...])
+            marks[t * part : (t + 1) * part, 0:part] = g.astype(BF)
+        for d in range(4):
+            for t in range(3):
+                start = pl.multiple_of(t * part + (s ^ d) * own, own)
+                totals[d][t * own : (t + 1) * own, :] = marks[pl.ds(start, own), 0:part]
+        ones = jnp.ones((8, 4 * block), BF)
+        g_bias[0:8, :] = nt(ones, d_q[...])
+        g_bias[8:16, :] = nt(ones, d_v[...])
+
+
+def attention_backward(place, grads, outs, packets, weights, shares, inverse, q_all, k_all, v_all):
+    part, block = grads[0].shape
+    length = 4 * block
+    heads = part // HEAD
+    own = part // 4
+    whole = lambda shape: pl.BlockSpec(shape, lambda h: (0,) * len(shape))
+    sd = jax.ShapeDtypeStruct
+    args = (*grads, *outs, *packets, weights, shares, inverse, q_all, k_all, v_all)
+    in_specs = [whole(a.shape) for a in args]
+    in_specs[13] = pl.BlockSpec((1, length, length), lambda h: (h, 0, 0))
+    results = [sd((part, block), BF)] * 4 + [sd((3 * own, part), BF)] * 4 + [sd((16, part), F32)]
+    return pl.pallas_call(
+        attention_back_kernel,
+        grid=(heads,),
+        out_shape=results,
+        in_specs=[smem()] + in_specs,
+        out_specs=[whole(o.shape) for o in results],
+        scratch_shapes=[
+            pltpu.VMEM((part, length), BF),
+            pltpu.VMEM((part, length), BF),
+            pltpu.VMEM((part, length), BF),
+            pltpu.VMEM((length, length), BF),
+        ],
+        compiler_params=pltpu.CompilerParams(vmem_limit_bytes=48 << 20),
+        name="attention_backward",
+    )(place, *args)
+
+
+def eighth_kernel(place, w_attn, w_inter, w_output, out, dense):
+    chip, core = place[1], place[2]
+    part = w_attn.shape[0]
+    width = w_attn.shape[1]
+    rows, cols = part // ROW_SPLIT, width // 2
+    for g in range(4):
+        dense[:, part * g : part * (g + 1)] = w_output[g]
+    take = aligned(chip, rows)
+    for half in range(2):
+
+        @pl.when(core == half)
+        def _():
+            lanes = slice(cols * half, cols * (half + 1))
+            out[0:rows, :] = w_attn[take, lanes]
+            out[rows : 2 * rows, :] = w_inter[chip, :, lanes]
+            out[2 * rows : 3 * rows, :] = dense[take, lanes]
+
+
+def rows_mean(v):
+    return jnp.mean(v, axis=1, keepdims=True)
+
+
+def middle_kernel(place, a0, a1, a2, a3, p0, p1, p2, p3, tokens, cotangent, *refs):
+    weights, refs = refs[:8], refs[8:]
+    (output, d_resid_one_out, b0, b1, b2, b3, keep_out, send_out, w_attn, w_inter, w_out, att, act, slope, grads, back) = refs
+    s, chip, core = place[0], place[1], place[2]
+    rows, width = tokens.shape
+    part = width // 4
+    piece_rows = part // ROW_SPLIT
+    half = width // 2
+
+    def place_weights(c, lanes):
+        for q in range(4):
+            for d in range(4):
+                ref, top = weights[c * 4 + q], 3 * piece_rows * d
+                start = pl.multiple_of((s ^ d) * part + (chip ^ q) * piece_rows, piece_rows)
+                w_attn[pl.ds(start, piece_rows), lanes] = ref[top : top + piece_rows, :]
+                w_inter[chip ^ q, aligned(s ^ d, piece_rows), lanes] = ref[top + piece_rows : top + 2 * piece_rows, :]
+                w_out[pl.ds(start, piece_rows), lanes] = ref[top + 2 * piece_rows : top + 3 * piece_rows, :]
+
+    for lane_half in range(2):
+        lanes = slice(half * lane_half, half * (lane_half + 1))
+
+        @pl.when(core == lane_half)
+        def _():
+            place_weights(0, lanes)
+
+        @pl.when(core != lane_half)
+        def _():
+            place_weights(1, lanes)
+
+    packets = (p0, p1, p2, p3)
+    base = part + 3 * piece_rows
+    vec = jnp.concatenate(
+        [
+            sum(p[base + VEC_ROWS * i : base + VEC_ROWS * (i + 1), :].astype(F32) for p in packets)
+            for i in range(width // rows)
+        ],
+        axis=1,
+    )
+    b_attn, gain_one, shift_one, b_output, gain_two, shift_two = (vec[i : i + 1, :] for i in range(6))
+
+    for d, ref in enumerate((a0, a1, a2, a3)):
+        att[aligned(s ^ d, part), :] = ref[...]
+    resid = tokens[...].astype(F32) + tn(att[...], w_attn[...]) + b_attn
+    centre = resid - rows_mean(resid)
+    inv_one = lax.rsqrt(rows_mean(centre * centre) + epsilon)
+    norm_one = centre * inv_one
+    first = norm_one * gain_one + shift_one
+    first_low = first.astype(BF)
+
+    outward = []
+    for g in range(4):
+        x = first_low[:, part * g : part * (g + 1)]
+        hidden = nn(x, w_inter[g]) + vec[8 + g : 9 + g, :]
+        phi = 0.5 + 0.5 * lax.erf(hidden * (0.5**0.5))
+        low = (hidden * phi).astype(BF)
+        act[g] = low
+        slope[g] = phi + hidden * (jnp.exp(-0.5 * hidden * hidden) * ((2.0 * math.pi) ** -0.5))
+        outward.append(nn(low, w_out[:, part * g : part * (g + 1)]))
+    resid = first + jnp.concatenate(outward, axis=1) + b_output
+    centre = resid - rows_mean(resid)
+    inv_two = lax.rsqrt(rows_mean(centre * centre) + epsilon)
+    norm_two = centre * inv_two
+    output[...] = (norm_two * gain_two + shift_two).astype(BF)
+
+    cot = cotangent[...].astype(F32)
+    total = lambda v: jnp.sum(v, axis=0, keepdims=True)
+    grad_gain_two, grad_shift_two = total(cot * norm_two), total(cot)
+    e_two = cot * gain_two
+    d_resid = inv_two * (e_two - rows_mean(e_two) - norm_two * rows_mean(e_two * norm_two))
+    grad_b_output = total(d_resid)
+    d_low = d_resid.astype(BF)
+    d_first, grad_b_inter = [], []
+    for g in range(4):
+        lanes = slice(part * g, part * (g + 1))
+        x = first_low[:, lanes]
+        dl = d_low[:, lanes]
+        grads[2 * width : 3 * width, lanes] = tn(act[g], dl).astype(BF)
+        d_hidden = nt(dl, w_out[:, lanes]) * slope[g]
+        grad_b_inter.append(total(d_hidden))
+        dh = d_hidden.astype(BF)
+        grads[width + part * g : width + part * (g + 1), :] = tn(x, dh).astype(BF)
+        d_first.append(nt(dh, w_inter[g]))
+    d_first = d_resid + jnp.concatenate(d_first, axis=1)
+    grad_gain_one, grad_shift_one = total(d_first * norm_one), total(d_first)
+    e_one = d_first * gain_one
+    d_one = inv_one * (e_one - rows_mean(e_one) - norm_one * rows_mean(e_one * norm_one))
+    d_resid_one_out[...] = d_one
+    grad_b_attn = total(d_one)
+    d_proj = d_one.astype(BF)
+    grads[0:width, :] = nn(att[...], d_proj).astype(BF)
+    back[...] = nt(w_attn[...], d_proj).astype(BF)
+    for d, ref in enumerate((b0, b1, b2, b3)):
+        ref[...] = back[aligned(s ^ d, part), :]
+
+    vec_grads = jnp.concatenate(
+        [grad_b_attn, grad_gain_one, grad_shift_one, grad_b_output, grad_gain_two, grad_shift_two]
+        + [jnp.zeros((2, width), F32)]
+        + grad_b_inter
+        + [jnp.zeros((4, width), F32)],
+        axis=0,
+    )
+    high = vec_grads.astype(BF)
+    rest = (vec_grads - high.astype(F32)).astype(BF)
+    for ref, flip in ((keep_out, 0), (send_out, 1)):
+        for lane_half in range(2):
+
+            @pl.when((core ^ flip) == lane_half)
+            def _():
+                lanes = slice(half * lane_half, half * (lane_half + 1))
+                for q in range(4):
+                    for d in range(4):
+                        top = (q * 4 + d) * 3 * piece_rows
+                        start = pl.multiple_of((s ^ d) * part + (chip ^ q) * piece_rows, piece_rows)
+                        inter = pl.multiple_of(width + (chip ^ q) * part + (s ^ d) * piece_rows, piece_rows)
+                        ref[top : top + piece_rows, :] = grads[pl.ds(start, piece_rows), lanes]
+                        ref[top + piece_rows : top + 2 * piece_rows, :] = grads[pl.ds(inter, piece_rows), lanes]
+                        ref[top + 2 * piece_rows : top + 3 * piece_rows, :] = grads[
+                            pl.ds(2 * width + start, piece_rows), lanes
+                        ]
+
+        top = 16 * 3 * piece_rows
+        ref[top : top + 16, :] = high[:, 0:half]
+        ref[top + 16 : top + 32, :] = high[:, half:width]
+        ref[top + 32 : top + 48, :] = rest[:, 0:half]
+        ref[top + 48 : top + 64, :] = rest[:, half:width]
+
+
+def join_kernel(place, *refs):
+    pieces, out = refs[:-1], refs[-1]
+    for i, piece in enumerate(pieces):
+        out[piece.shape[0] * i : piece.shape[0] * (i + 1), :] = piece[...]
+
+
+def split_low(v):
+    high = v.astype(BF)
+    return high, (v - high.astype(F32)).astype(BF)
+
+
+def tree(terms):
+    a, b, c, d = terms
+    return (a + b) + (c + d)
+
+
+def vec_of(ref, top):
+    return ref[top : top + 32, :].astype(F32) + ref[top + 32 : top + 64, :].astype(F32)
+
+
+def core_sum_kernel(place, mine, theirs, *outs):
+    piece = (mine.shape[0] - 64) // 4
+    high, rest = split_low(vec_of(mine, 4 * piece) + vec_of(theirs, 4 * piece))
+    for q, out in enumerate(outs):
+        rows = slice(piece * q, piece * (q + 1))
+        out[0:piece, :] = (mine[rows, :].astype(F32) + theirs[rows, :].astype(F32)).astype(BF)
+        out[piece : piece + 32, :] = high
+        out[piece + 32 : piece + 64, :] = rest
+
+
+def chip_sum_kernel(place, m0, m1, m2, m3, *outs):
+    whole = m0.shape[0] - 64
+    piece = whole // 4
+    parts = (m0, m1, m2, m3)
+    high, rest = split_low(tree(vec_of(m, whole) for m in parts))
+    for d, out in enumerate(outs):
+        rows = slice(piece * d, piece * (d + 1))
+        out[0:piece, :] = tree(m[rows, :].astype(F32) for m in parts).astype(BF)
+        out[piece : piece + 32, :] = high
+        out[piece + 32 : piece + 64, :] = rest
+
+
+def shard_sum_kernel(place, m0, m1, m2, m3, out, vec):
+    piece = m0.shape[0] - 64
+    parts = (m0, m1, m2, m3)
+    vec[...] = tree(vec_of(m, piece) for m in parts)
+    out[...] = tree(m[0:piece, :].astype(F32) for m in parts).astype(BF)
+
+
+def finish_kernel(place, vec, n0, n1, n2, n3, f0, f1, f2, f3, g_attn, g_inter, g_out, g_vec, g_lines, dense):
+    s, chip, core = place[0], place[1], place[2]
+    part, width = g_attn.shape
+    rows = part // ROW_SPLIT
+    half = width // 2
+
+    def place_half(pieces, lanes):
+        for q, ref in enumerate(pieces):
+            at = aligned(chip ^ q, rows)
+            g_attn[at, lanes] = ref[0:rows, :].astype(F32)
+            g_inter[chip ^ q, :, lanes] = ref[rows : 2 * rows, :].astype(F32)
+            dense[at, lanes] = ref[2 * rows : 3 * rows, :].astype(F32)
+
+    for lane_half in range(2):
+        lanes = slice(half * lane_half, half * (lane_half + 1))
+
+        @pl.when(core == lane_half)
+        def _():
+            place_half((n0, n1, n2, n3), lanes)
+
+        @pl.when(core != lane_half)
+        def _():
+            place_half((f0, f1, f2, f3), lanes)
+
+    for g in range(4):
+        g_out[g] = dense[:, part * g : part * (g + 1)]
+    full = jnp.concatenate([vec[0:16, :], vec[16:32, :]], axis=1)
+    for shard in range(4):
+
+        @pl.when(s == shard)
+        def _():
+            g_vec[...] = full[0:8, part * shard : part * (shard + 1)]
+            g_lines[...] = full[8 + shard : 9 + shard, :]
+
+
+def qkv_core_kernel(place, w0, w1, w2, w3, v0, v1, v2, v3, b_mine, b_theirs, out):
+    core = place[2]
+    rows = w0.shape[0]
+    mine, theirs = (w0, w1, w2, w3), (v0, v1, v2, v3)
+    for c in range(2):
+
+        @pl.when(core == c)
+        def _():
+            for i in range(2):
+                total = mine[2 * c + i][...].astype(F32) + theirs[2 * c + i][...].astype(F32)
+                out[rows * i : rows * (i + 1), :] = total.astype(BF)
+
+    high, rest = split_low(b_mine[...] + b_theirs[...])
+    out[2 * rows : 2 * rows + 16, :] = high
+    out[2 * rows + 16 : 2 * rows + 32, :] = rest
+
+
+def qkv_chip_kernel(place, m0, m1, m2, m3, out, bias):
+    rows = m0.shape[0] - 32
+    parts = (m0, m1, m2, m3)
+    out[...] = tree(m[0:rows, :].astype(F32) for m in parts).astype(BF)
+    bias[...] = tree(
+        m[rows : rows + 16, :].astype(F32) + m[rows + 16 : rows + 32, :].astype(F32) for m in parts
+    )
+
+
+def qkv_finish_kernel(place, near, far, bias, g_w, g_b):
+    s, core = place[0], place[2]
+    own = g_w.shape[2]
+    for c in range(2):
+
+        @pl.when(core == c)
+        def _():
+            for i in range(2):
+                for t in range(3):
+                    rows = slice((3 * i + t) * own, (3 * i + t + 1) * own)
+                    g_w[t, s ^ (2 * c + i)] = near[rows, :].astype(F32)
+                    g_w[t, s ^ (2 - 2 * c + i)] = far[rows, :].astype(F32)
+
+    g_b[0:1, :] = bias[0:1, :]
+    g_b[1:2, :] = bias[8:9, :]
+
+
+def tokens_kernel(place, d_resid, t0, t1, t2, t3, out, gathered):
+    s = place[0]
+    part = t0.shape[0]
+    for d, ref in enumerate((t0, t1, t2, t3)):
+        gathered[aligned(s ^ d, part), :] = ref[...]
+    out[...] = d_resid[...] + gathered[...].astype(F32).T
+
+
+def swap(x, axis, flip):
+    return lax.ppermute(x, axis, [(i, i ^ flip) for i in range(lax.axis_size(axis))])
+
+
+CHIPS = (2, 4, 6)
+
+
+def fast_body(
+    tokens, w_qkv, b_qv, w_attn, b_attn, ln1_gain, ln1_bias, w_inter, b_inter, w_output, b_output, ln2_gain, ln2_bias,
+    segment_ids, keep_mask, cotangent,
+):
+    sd = jax.ShapeDtypeStruct
+    rows, width = tokens.shape[1:]
+    part, half = width // 4, width // 2
+    own = part // 4
+    shard, rep = lax.axis_index("shard"), lax.axis_index("rep")
+    place = jnp.stack([shard, rep // 2, rep % 2]).astype(I32)
+    x = tokens.reshape(rows, width)
+
+    vectors = jnp.stack([b_attn, ln1_gain, ln1_bias, b_output, ln2_gain, ln2_bias, b_attn, b_attn])
+    height = part + 3 * own + VEC_ROWS * (width // rows)
+    *packets, _ = call(packet_kernel, [sd((height, rows), BF)] * 4 + [sd((width, rows), BF)], name="packets")(
+        place, x, w_qkv, vectors, b_inter.reshape(1, -1)
+    )
+    packets = [packets[0]] + [swap(packets[d], "shard", d) for d in (1, 2, 3)]
+
+    (eighth,) = call(eighth_kernel, [sd((3 * own, half), BF)], [pltpu.VMEM((part, width), BF)], name="eighth")(
+        place, w_attn, w_inter, w_output
+    )
+    eighths = [eighth] + [swap(eighth, "shard", d) for d in (1, 2, 3)]
+    (joined,) = call(join_kernel, [sd((12 * own, half), BF)], name="join")(place, *eighths)
+    near = [joined] + [swap(joined, "rep", c) for c in CHIPS]
+    weights = near + [swap(n, "rep", 1) for n in near]
+
+    *outs, w_all, shares, inverse, q_all, k_all, v_all = attention_forward(
+        place, packets, b_qv.T, segment_ids, keep_mask
+    )
+    attended = [outs[0]] + [swap(outs[d], "shard", d) for d in (1, 2, 3)]
+
+    total = 48 * own + 64
+    output, d_resid_one, *back, keep_part, send_part = call(
+        middle_kernel,
+        [sd((rows, width), BF), sd((rows, width), F32)] + [sd((part, rows), BF)] * 4 + [sd((total, half), BF)] * 2,
+        [
+            pltpu.VMEM((width, width), BF),
+            pltpu.VMEM((4, part, width), BF),
+            pltpu.VMEM((width, width), BF),
+            pltpu.VMEM((width, rows), BF),
+            pltpu.VMEM((4, rows, width), BF),
+            pltpu.VMEM((4, rows, width), F32),
+            pltpu.VMEM((3 * width, width), BF),
+            pltpu.VMEM((width, rows), BF),
+        ],
+        limit=56 << 20,
+        name="middle",
+    )(place, *attended, *packets, x, cotangent.reshape(rows, width), *weights)
+    d_attended = [back[0]] + [swap(back[d], "shard", d) for d in (1, 2, 3)]
+
+    by_chip = call(core_sum_kernel, [sd((12 * own + 64, half), BF)] * 4, name="core_sum")(
+        place, keep_part, swap(send_part, "rep", 1)
+    )
+    by_shard = call(chip_sum_kernel, [sd((3 * own + 64, half), BF)] * 4, name="chip_sum")(
+        place, by_chip[0], *(swap(by_chip[q], "rep", c) for q, c in ((1, 2), (2, 4), (3, 6)))
+    )
+    summed, vec = call(shard_sum_kernel, [sd((3 * own, half), BF), sd((32, half), F32)], name="shard_sum")(
+        place, by_shard[0], *(swap(by_shard[d], "shard", d) for d in (1, 2, 3))
+    )
+    near = [summed] + [swap(summed, "rep", c) for c in CHIPS]
+    g_attn, g_inter, g_out, g_vec, g_lines = call(
+        finish_kernel,
+        [sd((part, width), F32), sd((4, own, width), F32), sd((4, part, part), F32), sd((8, part), F32), sd((1, width), F32)],
+        [pltpu.VMEM((part, width), F32)],
+        name="finish",
+    )(place, vec, *near, *(swap(n, "rep", 1) for n in near))
+
+    results = attention_backward(
+        place, d_attended, outs, packets, w_all, shares, inverse, q_all, k_all, v_all
+    )
+    d_parts, w_parts, g_bias = results[:4], results[4:8], results[8]
+    d_parts = [d_parts[0]] + [swap(d_parts[d], "shard", d) for d in (1, 2, 3)]
+    w_parts = [w_parts[0]] + [swap(w_parts[d], "shard", d) for d in (1, 2, 3)]
+    (d_tokens,) = call(tokens_kernel, [sd((rows, width), F32)], [pltpu.VMEM((width, rows), BF)], name="d_tokens")(
+        place, d_resid_one, *d_parts
+    )
+    (mine,) = call(qkv_core_kernel, [sd((6 * own + 32, part), BF)], name="qkv_core")(
+        place, *w_parts, *(swap(w, "rep", 1) for w in w_parts), g_bias, swap(g_bias, "rep", 1)
+    )
+    half_sum, bias_sum = call(qkv_chip_kernel, [sd((6 * own, part), BF), sd((16, part), F32)], name="qkv_chip")(
+        place, mine, *(swap(mine, "rep", c) for c in CHIPS)
+    )
+    g_qkv, g_bqv = call(qkv_finish_kernel, [sd((3, 4, own, part), F32), sd((2, part), F32)], name="qkv_finish")(
+        place, half_sum, swap(half_sum, "rep", 1), bias_sum
+    )
+    return (
+        output[None],
+        d_tokens[None],
+        g_qkv,
+        g_bqv,
+        g_attn,
+        g_vec[0],
+        g_vec[1],
+        g_vec[2],
+        g_inter,
+        g_lines[0],
+        g_out,
+        g_vec[3],
+        g_vec[4],
+        g_vec[5],
+    )
+
+
+def fits_fast(mesh):
+    return mesh.shape["shard"] == GROUPS == 4 and mesh.shape["rep"] == 8
+
+
 def solution(mesh):
     in_specs = (
         P("rep", "shard", None),
@@ -408,4 +1059,5 @@
         P("shard"),
         P("shard"),
     )
-    return jax.shard_map(body, mesh=mesh, in_specs=in_specs, out_specs=out_specs, check_vma=False)
+    plan = fast_body if fits_fast(mesh) else body
+    return jax.shard_map(plan, mesh=mesh, in_specs=in_specs, out_specs=out_specs, check_vma=False)

time: 796 us -> 166 us (0.21)
  waiting for transfers between devices: 495 us -> 52.1 us
  blocking collectives: 108 us -> 0 us
  matrix products: 94.9 us -> 0 us
  starting transfers between devices: 0.53 us -> 56.9 us
  Pallas kernels: 0 us -> 47.8 us
  local copies, waits for them, and re-layouts: 42.8 us -> 7.18 us
  other arithmetic: 34.5 us -> 0.68 us
  between operations: 17.3 us -> 1.25 us
    reduce_scatter x5 -> x0, waiting for transfers between devices: 279 us -> none  [the longest x1 62.1 us: body(): lax.psum_scatter(d_out_w, 'shard', scatter_dimension=1, tiled=True)]
    dot_general x54 -> x0, matrix products: 94.9 us -> none  [the longest x12 21.5 us: masked_scores(): jnp.einsum('hqd,hkd->hqk', query_blk, key_piece, preferred_element_type=j...]
    unnamed x15 -> x0, waiting for transfers between devices: 87.8 us -> none
    all_gather x5 -> x0, waiting for transfers between devices: 84.8 us -> none  [the longest x1 28.5 us: body(): lax.all_gather(w_inter, 'shard', axis=1, tiled=True)]
    ppermute x0 -> x48, starting transfers between devices: none -> 56.9 us  [swap(): lax.ppermute(x, axis, [(i, i ^ flip) for i in range(lax.axis_size(axis))])]
    ppermute x0 -> x48, waiting for transfers between devices: none -> 52.1 us  [swap(): lax.ppermute(x, axis, [(i, i ^ flip) for i in range(lax.axis_size(axis))])]
    all_gather x3 -> x0, blocking collectives: 49.6 us -> none  [the longest x1 25.6 us: body(): lax.all_gather(w_qkv, 'shard', axis=2, tiled=True)]
    pallas_call x0 -> x14, Pallas kernels: none -> 47.8 us  [the longest x12 23.4 us: go(): pl.pallas_call(kernel, out_shape=outs, in_specs=[smem()] + vmem(len(args)...]
  transfers between devices with their start and end apart: 13 -> 48, of which waited for: 11 -> 16; matrix products, arithmetic and copies ran while one was open for 8% -> 0% of each run, Pallas kernels for 0% -> 19%
where the time goes in v1:
time: 166 us
  starting transfers between devices  56.9 us (34%)
  waiting for transfers between devices  52.1 us (31%)
  Pallas kernels  47.8 us (29%)
  local copies, waits for them, and re-layouts  7.18 us (4%)
    ppermute x48, starting transfers between devices, swap(): lax.ppermute(x, axis, [(i, i ^ flip) for i in range(lax.axis_size(axis))])  56.9 us
    ppermute x48, waiting for transfers between devices, swap(): lax.ppermute(x, axis, [(i, i ^ flip) for i in range(lax.axis_size(axis))])  52.1 us
    pallas_call x12, Pallas kernels, go(): pl.pallas_call(kernel, out_shape=outs, in_specs=[smem()] + vmem(len(args)...  23.4 us
    pallas_call x1, Pallas kernels, attention_forward(): pl.pallas_call(attention_kernel, grid=(heads,), out_shape=outs, in_specs=...  13 us
    pallas_call x1, Pallas kernels, attention_backward(): pl.pallas_call(attention_back_kernel, grid=(heads,), out_shape=results, i...  11.5 us
    unnamed x83, local copies, waits for them, and re-layouts  6.53 us
  transfers between devices with their start and end apart: 48, of which 16 were waited for; matrix products, arithmetic and copies ran while one was open for 0% of the time, Pallas kernels for 19%

profile of v1, /device:TPU:0, one launch (start us, length us, event | category | flops | bytes accessed | tf_op | source)
XLA Modules:
  0.0 165.9 jit_solution(2884916574693577938)
XLA Ops:
  0.8 1.0 copy-done.14
  1.8 1.0 copy-done.16
  2.7 1.0 copy-done.17
  3.8 0.7 eighth.1.refs_0_
  4.5 5.1 %collective-permute-start.8 = (bf16[144,384]{1,0:T(8,128)(2,1)S(1)}, bf16[144,384]{1,0:T(8,128)(2,1)S(1)}, u32[]{:S(2)}, u32[]{:S(2)}) collective-permute-start(bf16[144,384]{1,0:T(8,128)(2,1)S(1)} %eighth.1.refs_0_), channel_id=1, source_target_pairs={{0,3},{1,2},{2,1},{3,0},{4,7},{5,6},{6,5},{7,4},{8,11},{9,10},{10,... | collective-permute-start | bytes 331784 | tf_op jit(solution)/shard_map/ppermute | solution.py:913
  9.6 0.6 collective-permute-start.6
  10.2 3.3 %collective-permute-done.8.refs_3_ = bf16[144,384]{1,0:T(8,128)(2,1)S(1)} collective-permute-done((bf16[144,384]{1,0:T(8,128)(2,1)S(1)}, bf16[144,384]{1,0:T(8,128)(2,1)S(1)}, u32[]{:S(2)}, u32[]{:S(2)}) %collective-permute-start.8) | collective-permute-done | bytes 110624 | tf_op jit(solution)/shard_map/ppermute | solution.py:913
  13.6 5.3 %collective-permute-done.7.refs_2_ = bf16[144,384]{1,0:T(8,128)(2,1)S(1)} collective-permute-done((bf16[144,384]{1,0:T(8,128)(2,1)S(1)}, bf16[144,384]{1,0:T(8,128)(2,1)S(1)}, u32[]{:S(2)}, u32[]{:S(2)}) %collective-permute-start.7) | collective-permute-done | bytes 110624 | tf_op jit(solution)/shard_map/ppermute | solution.py:913
  18.9 0.6 join.1.refs_0_
  19.5 2.5 %collective-permute-start.11 = (bf16[576,384]{1,0:T(8,128)(2,1)S(1)}, bf16[576,384]{1,0:T(8,128)(2,1)S(1)}, u32[]{:S(2)}, u32[]{:S(2)}) collective-permute-start(bf16[576,384]{1,0:T(8,128)(2,1)S(1)} %join.1.refs_0_), channel_id=1, source_target_pairs={{0,24},{4,28},{8,16},{12,20},{16,8},{20,12},{24,0},{28,4},{1,25},{... | collective-permute-start | bytes 1327112 | tf_op jit(solution)/shard_map/ppermute | solution.py:913
  22.5 0.5 collective-permute-start.9
  23.3 1.5 packets.1
  25.1 2.8 %collective-permute-start.1 = (bf16[384,256]{1,0:T(8,128)(2,1)S(1)}, bf16[384,256]{1,0:T(8,128)(2,1)S(1)}, u32[]{:S(2)}, u32[]{:S(2)}) collective-permute-start(bf16[384,256]{1,0:T(8,128)(2,1)S(1)} %get-tuple-element.66), channel_id=1, source_target_pairs={{0,2},{1,3},{2,0},{3,1},{4,6},{5,7},{6,4},{7,5},{8,10},{9,11},{10,... | collective-permute-start | bytes 589832 | tf_op jit(solution)/shard_map/ppermute | solution.py:913
  27.9 6.0 %collective-permute-done.p1 = bf16[384,256]{1,0:T(8,128)(2,1)S(1)} collective-permute-done((bf16[384,256]{1,0:T(8,128)(2,1)S(1)}, bf16[384,256]{1,0:T(8,128)(2,1)S(1)}, u32[]{:S(2)}, u32[]{:S(2)}) %collective-permute-start) | collective-permute-done | bytes 196640 | tf_op jit(solution)/shard_map/ppermute | solution.py:913
  33.9 1.6 collective-permute-start.2
  36.0 5.2 %collective-permute-done.10.refs_2_ = bf16[576,384]{1,0:T(8,128)(2,1)S(1)} collective-permute-done((bf16[576,384]{1,0:T(8,128)(2,1)S(1)}, bf16[576,384]{1,0:T(8,128)(2,1)S(1)}, u32[]{:S(2)}, u32[]{:S(2)}) %collective-permute-start.10) | collective-permute-done | bytes 442400 | tf_op jit(solution)/shard_map/ppermute | solution.py:913
  41.9 13.0 %attention_forward.1 = (bf16[192,256]{1,0:T(8,128)(2,1)S(1)}, bf16[192,256]{1,0:T(8,128)(2,1)S(1)}, bf16[192,256]{1,0:T(8,128)(2,1)S(1)}, bf16[192,256]{1,0:T(8,...) custom-call(s32[3]{0:T(128)S(1)} %pad_add_fusion.place, ...), custom_call_target="tpu_custom_call" | custom-call | tf_op jit(solution)/shard_map/attention_forward/pallas_call | solution.py:538
  54.9 0.6 copy-done.12
  55.5 2.1 %collective-permute-start.3 = (bf16[192,256]{1,0:T(8,128)(2,1)S(1)}, bf16[192,256]{1,0:T(8,128)(2,1)S(1)}, u32[]{:S(2)}, u32[]{:S(2)}) collective-permute-start(bf16[192,256]{1,0:T(8,128)(2,1)S(1)} %get-tuple-element.69.o1), channel_id=1, source_target_pairs={{0,1},{1,0},{2,3},{3,2},{4,5},{5,4},{6,7},{7,6},{8,9},{9,8},{10,11... | collective-permute-start | bytes 294920 | tf_op jit(solution)/shard_map/ppermute | solution.py:913
  57.6 2.7 %collective-permute-done.3.a1 = bf16[192,256]{1,0:T(8,128)(2,1)S(1)} collective-permute-done((bf16[192,256]{1,0:T(8,128)(2,1)S(1)}, bf16[192,256]{1,0:T(8,128)(2,1)S(1)}, u32[]{:S(2)}, u32[]{:S(2)}) %collective-permute-start.3) | collective-permute-done | bytes 98336 | tf_op jit(solution)/shard_map/ppermute | solution.py:913
  60.3 2.8 %collective-permute-start.4 = (bf16[192,256]{1,0:T(8,128)(2,1)S(1)}, bf16[192,256]{1,0:T(8,128)(2,1)S(1)}, u32[]{:S(2)}, u32[]{:S(2)}) collective-permute-start(bf16[192,256]{1,0:T(8,128)(2,1)S(1)} %get-tuple-element.70.o2), channel_id=1, source_target_pairs={{0,2},{1,3},{2,0},{3,1},{4,6},{5,7},{6,4},{7,5},{8,10},{9,11},{10,... | collective-permute-start | bytes 294920 | tf_op jit(solution)/shard_map/ppermute | solution.py:913
  63.1 2.7 %collective-permute-done.4.a2 = bf16[192,256]{1,0:T(8,128)(2,1)S(1)} collective-permute-done((bf16[192,256]{1,0:T(8,128)(2,1)S(1)}, bf16[192,256]{1,0:T(8,128)(2,1)S(1)}, u32[]{:S(2)}, u32[]{:S(2)}) %collective-permute-start.4) | collective-permute-done | bytes 98336 | tf_op jit(solution)/shard_map/ppermute | solution.py:913
  65.9 2.2 %collective-permute-start.5 = (bf16[192,256]{1,0:T(8,128)(2,1)S(1)}, bf16[192,256]{1,0:T(8,128)(2,1)S(1)}, u32[]{:S(2)}, u32[]{:S(2)}) collective-permute-start(bf16[192,256]{1,0:T(8,128)(2,1)S(1)} %get-tuple-element.71.o3), channel_id=1, source_target_pairs={{0,3},{1,2},{2,1},{3,0},{4,7},{5,6},{6,5},{7,4},{8,11},{9,10},{10,... | collective-permute-start | bytes 294920 | tf_op jit(solution)/shard_map/ppermute | solution.py:913
  68.1 4.3 %collective-permute-done.5.a3 = bf16[192,256]{1,0:T(8,128)(2,1)S(1)} collective-permute-done((bf16[192,256]{1,0:T(8,128)(2,1)S(1)}, bf16[192,256]{1,0:T(8,128)(2,1)S(1)}, u32[]{:S(2)}, u32[]{:S(2)}) %collective-permute-start.5) | collective-permute-done | bytes 98336 | tf_op jit(solution)/shard_map/ppermute | solution.py:913
  73.0 11.8 %middle.1 = (bf16[256,768]{1,0:T(8,128)(2,1)}, f32[256,768]{1,0:T(8,128)}, bf16[192,256]{1,0:T(8,128)(2,1)}, bf16[192,256]{1,0:T(8,128)(2,1)}, bf16[192,256]{1,0...) custom-call(s32[3]{0:T(128)} %copy-done.18, ...), custom_call_target="tpu_custom_call" | custom-call | tf_op jit(solution)/shard_map/middle/pallas_call | solution.py:411
  85.0 4.0 %collective-permute-done.34.theirs = bf16[2368,384]{1,0:T(8,128)(2,1)S(1)} collective-permute-done((bf16[2368,384]{1,0:T(8,128)(2,1)}, bf16[2368,384]{1,0:T(8,128)(2,1)S(1)}, u32[]{:S(2)}, u32[]{:S(2)}) %collective-permute-start.34) | collective-permute-done | bytes 1818656 | tf_op jit(solution)/shard_map/ppermute | solution.py:913
  88.9 1.5 copy-done
  90.4 0.7 copy-done.19
  91.1 1.0 core_sum.1
  92.1 1.6 collective-permute-start.35
  93.7 1.4 collective-permute-start.36
  95.1 0.6 collective-permute-start.37
  95.7 1.1 collective-permute-start.16
  96.8 1.7 %collective-permute-start.17 = (bf16[192,256]{1,0:T(8,128)(2,1)S(1)}, bf16[192,256]{1,0:T(8,128)(2,1)S(1)}, u32[]{:S(2)}, u32[]{:S(2)}) collective-permute-start(bf16[192,256]{1,0:T(8,128)(2,1)S(1)} %copy-done.33), channel_id=1, source_target_pairs={{0,2},{1,3},{2,0},{3,1},{4,6},{5,7},{6,4},{7,5},{8,10},{9,11},{10,... | collective-permute-start | bytes 294920 | tf_op jit(solution)/shard_map/ppermute | solution.py:913
  98.5 2.8 %collective-permute-done.16.g1 = bf16[192,256]{1,0:T(8,128)(2,1)S(1)} collective-permute-done((bf16[192,256]{1,0:T(8,128)(2,1)S(1)}, bf16[192,256]{1,0:T(8,128)(2,1)S(1)}, u32[]{:S(2)}, u32[]{:S(2)}) %collective-permute-start.16) | collective-permute-done | bytes 98336 | tf_op jit(solution)/shard_map/ppermute | solution.py:913
  101.3 2.2 %collective-permute-start.18 = (bf16[192,256]{1,0:T(8,128)(2,1)S(1)}, bf16[192,256]{1,0:T(8,128)(2,1)S(1)}, u32[]{:S(2)}, u32[]{:S(2)}) collective-permute-start(bf16[192,256]{1,0:T(8,128)(2,1)S(1)} %copy-done.32), channel_id=1, source_target_pairs={{0,3},{1,2},{2,1},{3,0},{4,7},{5,6},{6,5},{7,4},{8,11},{9,10},{10,... | collective-permute-start | bytes 294920 | tf_op jit(solution)/shard_map/ppermute | solution.py:913
  103.5 1.7 %collective-permute-done.17.g2 = bf16[192,256]{1,0:T(8,128)(2,1)S(1)} collective-permute-done((bf16[192,256]{1,0:T(8,128)(2,1)S(1)}, bf16[192,256]{1,0:T(8,128)(2,1)S(1)}, u32[]{:S(2)}, u32[]{:S(2)}) %collective-permute-start.17) | collective-permute-done | bytes 98336 | tf_op jit(solution)/shard_map/ppermute | solution.py:913
  105.2 2.5 %collective-permute-done.18.g3 = bf16[192,256]{1,0:T(8,128)(2,1)S(1)} collective-permute-done((bf16[192,256]{1,0:T(8,128)(2,1)S(1)}, bf16[192,256]{1,0:T(8,128)(2,1)S(1)}, u32[]{:S(2)}, u32[]{:S(2)}) %collective-permute-start.18) | collective-permute-done | bytes 98336 | tf_op jit(solution)/shard_map/ppermute | solution.py:913
  107.8 11.5 %attention_backward.1 = (bf16[192,256]{1,0:T(8,128)(2,1)S(1)}, bf16[192,256]{1,0:T(8,128)(2,1)S(1)}, bf16[192,256]{1,0:T(8,128)(2,1)S(1)}, bf16[192,256]{1,0:T(8...) custom-call(s32[3]{0:T(128)S(1)} %copy-done.20, ...), custom_call_target="tpu_custom_call" | custom-call | tf_op jit(solution)/shard_map/attention_backward/pallas_call | solution.py:611
  119.3 2.8 %collective-permute-start.23 = (bf16[144,192]{1,0:T(8,128)(2,1)S(1)}, bf16[144,192]{1,0:T(8,128)(2,1)S(1)}, u32[]{:S(2)}, u32[]{:S(2)}) collective-permute-start(bf16[144,192]{1,0:T(8,128)(2,1)S(1)} %get-tuple-element.90), channel_id=1, source_target_pairs={{0,2},{1,3},{2,0},{3,1},{4,6},{5,7},{6,4},{7,5},{8,10},{9,11},{10,... | collective-permute-start | bytes 165896 | tf_op jit(solution)/shard_map/ppermute | solution.py:913
  122.1 0.8 chip_sum.1
  122.9 0.7 collective-permute-start.38
  123.6 1.5 collective-permute-start.39
  125.1 1.2 collective-permute-done.29.b_theirs
  126.3 2.3 %collective-permute-start.24 = (bf16[144,192]{1,0:T(8,128)(2,1)S(1)}, bf16[144,192]{1,0:T(8,128)(2,1)S(1)}, u32[]{:S(2)}, u32[]{:S(2)}) collective-permute-start(bf16[144,192]{1,0:T(8,128)(2,1)S(1)} %get-tuple-element.91), channel_id=1, source_target_pairs={{0,3},{1,2},{2,1},{3,0},{4,7},{5,6},{6,5},{7,4},{8,11},{9,10},{10,... | collective-permute-start | bytes 165896 | tf_op jit(solution)/shard_map/ppermute | solution.py:913
  129.1 4.4 %collective-permute-done.24.w3 = bf16[144,192]{1,0:T(8,128)(2,1)S(1)} collective-permute-done((bf16[144,192]{1,0:T(8,128)(2,1)S(1)}, bf16[144,192]{1,0:T(8,128)(2,1)S(1)}, u32[]{:S(2)}, u32[]{:S(2)}) %collective-permute-start.24) | collective-permute-done | bytes 55328 | tf_op jit(solution)/shard_map/ppermute | solution.py:913
  133.5 0.5 collective-permute-start.28
  134.0 1.6 collective-permute-start.40
  135.6 0.6 qkv_core.1.m0
  136.2 2.8 %collective-permute-start.32 = (bf16[320,192]{1,0:T(8,128)(2,1)S(1)}, bf16[320,192]{1,0:T(8,128)(2,1)S(1)}, u32[]{:S(2)}, u32[]{:S(2)}) collective-permute-start(bf16[320,192]{1,0:T(8,128)(2,1)S(1)} %qkv_core.1.m0), channel_id=1, source_target_pairs={{0,24},{4,28},{8,16},{12,20},{16,8},{20,12},{24,0},{28,4},{1,25},{... | collective-permute-start | bytes 368648 | tf_op jit(solution)/shard_map/ppermute | solution.py:913
  139.8 2.3 %collective-permute-start.19 = (bf16[192,256]{1,0:T(8,128)(2,1)S(1)}, bf16[192,256]{1,0:T(8,128)(2,1)S(1)}, u32[]{:S(2)}, u32[]{:S(2)}) collective-permute-start(bf16[192,256]{1,0:T(8,128)(2,1)S(1)} %get-tuple-element.85), channel_id=1, source_target_pairs={{0,1},{1,0},{2,3},{3,2},{4,5},{5,4},{6,7},{7,6},{8,9},{9,8},{10,11... | collective-permute-start | bytes 294920 | tf_op jit(solution)/shard_map/ppermute | solution.py:913
  142.1 0.6 shard_sum.1
  142.7 2.6 %collective-permute-start.43 = (bf16[144,384]{1,0:T(8,128)(2,1)S(1)}, bf16[144,384]{1,0:T(8,128)(2,1)S(1)}, u32[]{:S(2)}, u32[]{:S(2)}) collective-permute-start(bf16[144,384]{1,0:T(8,128)(2,1)S(1)} %get-tuple-element.108.n0), channel_id=1, source_target_pairs={{0,24},{4,28},{8,16},{12,20},{16,8},{20,12},{24,0},{28,4},{1,25},{... | collective-permute-start | bytes 331784 | tf_op jit(solution)/shard_map/ppermute | solution.py:913
  145.3 1.0 collective-permute-start.42
  146.3 1.5 collective-permute-start.41
  148.2 2.0 %collective-permute-start.20 = (bf16[192,256]{1,0:T(8,128)(2,1)S(1)}, bf16[192,256]{1,0:T(8,128)(2,1)S(1)}, u32[]{:S(2)}, u32[]{:S(2)}) collective-permute-start(bf16[192,256]{1,0:T(8,128)(2,1)S(1)} %get-tuple-element.86), channel_id=1, source_target_pairs={{0,2},{1,3},{2,0},{3,1},{4,6},{5,7},{6,4},{7,5},{8,10},{9,11},{10,... | collective-permute-start | bytes 294920 | tf_op jit(solution)/shard_map/ppermute | solution.py:913
  150.3 2.1 %collective-permute-start.21 = (bf16[192,256]{1,0:T(8,128)(2,1)S(1)}, bf16[192,256]{1,0:T(8,128)(2,1)S(1)}, u32[]{:S(2)}, u32[]{:S(2)}) collective-permute-start(bf16[192,256]{1,0:T(8,128)(2,1)S(1)} %get-tuple-element.87), channel_id=1, source_target_pairs={{0,3},{1,2},{2,1},{3,0},{4,7},{5,6},{6,5},{7,4},{8,11},{9,10},{10,... | collective-permute-start | bytes 294920 | tf_op jit(solution)/shard_map/ppermute | solution.py:913
  152.4 0.6 qkv_chip.1
  153.0 5.3 %collective-permute-done.20.t2 = bf16[192,256]{1,0:T(8,128)(2,1)S(1)} collective-permute-done((bf16[192,256]{1,0:T(8,128)(2,1)S(1)}, bf16[192,256]{1,0:T(8,128)(2,1)S(1)}, u32[]{:S(2)}, u32[]{:S(2)}) %collective-permute-start.20) | collective-permute-done | bytes 98336 | tf_op jit(solution)/shard_map/ppermute | solution.py:913
  159.5 1.6 d_tokens.1
  161.1 1.4 qkv_finish.1
  162.5 2.1 %finish.1 = (f32[192,768]{1,0:T(8,128)}, f32[4,48,768]{2,1,0:T(8,128)}, f32[4,192,192]{2,1,0:T(8,128)}, f32[8,192]{1,0:T(8,128)S(1)}, f32[1,768]{1,0:T(1,128)S(1)}) custom-call(s32[3]{0:T(128)S(1)} %copy-done.20, f32[32,384]{1,0:T(8,128)S(1)} %get-tuple-element.107.vec, bf16[144,384]{1,0:T(8,128)(2,1)S(1)} %get-tuple-element.108.n0, ...), custom_call_target="tpu_custom_call" | custom-call | tf_op jit(solution)/shard_map/finish/pallas_call | solution.py:411
  164.7 0.6 fusion
  165.3 0.6 reduce
  (140 shorter events, 5.7 us)
Async XLA Ops:
  0.6 22.6 %copy-start.10 = (bf16[1,256,768]{2,1,0:T(8,128)(2,1)S(1)}, bf16[1,256,768]{2,1,0:T(8,128)(2,1)}, u32[]{:S(2)}) copy-start(bf16[1,256,768]{2,1,0:T(8,128)(2,1)} %param.16) | copy-start | bytes 1179652
  3.7 68.7 %copy-start.18 = (s32[3]{0:T(128)}, s32[3]{0:T(128)S(1)}, u32[]{:S(2)}) copy-start(s32[3]{0:T(128)S(1)} %pad_add_fusion.place) | copy-start | bytes 40
  3.8 19.4 %copy-start.30 = (bf16[768]{0:T(1024)(128)(2,1)S(1)}, bf16[768]{0:T(1024)(128)(2,1)}, u32[]{:S(2)}) copy-start(bf16[768]{0:T(1024)(128)(2,1)} %param.24) | copy-start | bytes 4612
  3.8 19.5 %copy-start.15 = (bf16[3,4,48,192]{3,2,1,0:T(8,128)(2,1)S(1)}, bf16[3,4,48,192]{3,2,1,0:T(8,128)(2,1)}, u32[]{:S(2)}) copy-start(bf16[3,4,48,192]{3,2,1,0:T(8,128)(2,1)} %w_qkv.1) | copy-start | bytes 663556
  3.8 37.9 %copy-start.31 = (bf16[2,192]{1,0:T(2,128)(2,1)S(1)}, bf16[2,192]{1,0:T(2,128)(2,1)}, u32[]{:S(2)}) copy-start(bf16[2,192]{1,0:T(2,128)(2,1)} %param.18) | copy-start | bytes 2308
  3.8 38.1 %copy-start.22 = (s32[1,1024]{1,0:T(1,128)S(1)}, s32[1,1024]{1,0:T(1,128)}, u32[]{:S(2)}) copy-start(s32[1,1024]{1,0:T(1,128)} %segments.1) | copy-start | bytes 12292
  3.8 38.1 %copy-start.23 = (s32[1,1024]{1,0:T(1,128)S(1)}, s32[1,1024]{1,0:T(1,128)}, u32[]{:S(2)}) copy-start(s32[1,1024]{1,0:T(1,128)} %keep.1) | copy-start | bytes 12292
  4.5 9.1 %collective-permute-start.8 = (bf16[144,384]{1,0:T(8,128)(2,1)S(1)}, bf16[144,384]{1,0:T(8,128)(2,1)S(1)}, u32[]{:S(2)}, u32[]{:S(2)}) collective-permute-start(bf16[144,384]{1,0:T(8,128)(2,1)S(1)} %eighth.1.refs_0_), channel_id=1, source_target_pairs={{0,3},{1,2},{2,1},{3,0},{4,7},{5,6},{6,5},{7,4},{8,11},{9,10},{10,... | collective-permute-start | bytes 331784 | tf_op jit(solution)/shard_map/ppermute | solution.py:913
  9.6 9.3 %collective-permute-start.7 = (bf16[144,384]{1,0:T(8,128)(2,1)S(1)}, bf16[144,384]{1,0:T(8,128)(2,1)S(1)}, u32[]{:S(2)}, u32[]{:S(2)}) collective-permute-start(bf16[144,384]{1,0:T(8,128)(2,1)S(1)} %eighth.1.refs_0_), channel_id=1, source_target_pairs={{0,2},{1,3},{2,0},{3,1},{4,6},{5,7},{6,4},{7,5},{8,10},{9,11},{10,... | collective-permute-start | bytes 331784 | tf_op jit(solution)/shard_map/ppermute | solution.py:913
  9.6 9.3 %collective-permute-start.6 = (bf16[144,384]{1,0:T(8,128)(2,1)S(1)}, bf16[144,384]{1,0:T(8,128)(2,1)S(1)}, u32[]{:S(2)}, u32[]{:S(2)}) collective-permute-start(bf16[144,384]{1,0:T(8,128)(2,1)S(1)} %eighth.1.refs_0_), channel_id=1, source_target_pairs={{0,1},{1,0},{2,3},{3,2},{4,5},{5,4},{6,7},{7,6},{8,9},{9,8},{10,11... | collective-permute-start | bytes 331784 | tf_op jit(solution)/shard_map/ppermute | solution.py:913
  19.5 52.9 %copy-start.1 = (bf16[576,384]{1,0:T(8,128)(2,1)}, bf16[576,384]{1,0:T(8,128)(2,1)S(1)}, u32[]{:S(2)}) copy-start(bf16[576,384]{1,0:T(8,128)(2,1)S(1)} %join.1.refs_0_) | copy-start | bytes 1327108
  19.5 16.0 %collective-permute-start.11 = (bf16[576,384]{1,0:T(8,128)(2,1)S(1)}, bf16[576,384]{1,0:T(8,128)(2,1)S(1)}, u32[]{:S(2)}, u32[]{:S(2)}) collective-permute-start(bf16[576,384]{1,0:T(8,128)(2,1)S(1)} %join.1.refs_0_), channel_id=1, source_target_pairs={{0,24},{4,28},{8,16},{12,20},{16,8},{20,12},{24,0},{28,4},{1,25},{... | collective-permute-start | bytes 1327112 | tf_op jit(solution)/shard_map/ppermute | solution.py:913
  22.0 19.2 %collective-permute-start.10 = (bf16[576,384]{1,0:T(8,128)(2,1)S(1)}, bf16[576,384]{1,0:T(8,128)(2,1)S(1)}, u32[]{:S(2)}, u32[]{:S(2)}) collective-permute-start(bf16[576,384]{1,0:T(8,128)(2,1)S(1)} %join.1.refs_0_), channel_id=1, source_target_pairs={{0,16},{4,20},{8,24},{12,28},{16,0},{20,4},{24,8},{28,12},{1,17},{... | collective-permute-start | bytes 1327112 | tf_op jit(solution)/shard_map/ppermute | solution.py:913
  22.5 18.7 %collective-permute-start.9 = (bf16[576,384]{1,0:T(8,128)(2,1)S(1)}, bf16[576,384]{1,0:T(8,128)(2,1)S(1)}, u32[]{:S(2)}, u32[]{:S(2)}) collective-permute-start(bf16[576,384]{1,0:T(8,128)(2,1)S(1)} %join.1.refs_0_), channel_id=1, source_target_pairs={{0,8},{4,12},{8,0},{12,4},{16,24},{20,28},{24,16},{28,20},{1,9},{5... | collective-permute-start | bytes 1327112 | tf_op jit(solution)/shard_map/ppermute | solution.py:913
  24.8 47.7 %copy-start.2 = (bf16[384,256]{1,0:T(8,128)(2,1)}, bf16[384,256]{1,0:T(8,128)(2,1)S(1)}, u32[]{:S(2)}) copy-start(bf16[384,256]{1,0:T(8,128)(2,1)S(1)} %get-tuple-element.64.p0) | copy-start | bytes 589828
  24.8 9.1 %collective-permute-start = (bf16[384,256]{1,0:T(8,128)(2,1)S(1)}, bf16[384,256]{1,0:T(8,128)(2,1)S(1)}, u32[]{:S(2)}, u32[]{:S(2)}) collective-permute-start(bf16[384,256]{1,0:T(8,128)(2,1)S(1)} %get-tuple-element.65), channel_id=1, source_target_pairs={{0,1},{1,0},{2,3},{3,2},{4,5},{5,4},{6,7},{7,6},{8,9},{9,8},{10,11... | collective-permute-start | bytes 589832 | tf_op jit(solution)/shard_map/ppermute | solution.py:913
  25.1 10.4 %collective-permute-start.1 = (bf16[384,256]{1,0:T(8,128)(2,1)S(1)}, bf16[384,256]{1,0:T(8,128)(2,1)S(1)}, u32[]{:S(2)}, u32[]{:S(2)}) collective-permute-start(bf16[384,256]{1,0:T(8,128)(2,1)S(1)} %get-tuple-element.66), channel_id=1, source_target_pairs={{0,2},{1,3},{2,0},{3,1},{4,6},{5,7},{6,4},{7,5},{8,10},{9,11},{10,... | collective-permute-start | bytes 589832 | tf_op jit(solution)/shard_map/ppermute | solution.py:913
  33.9 38.6 %copy-start.4 = (bf16[384,256]{1,0:T(8,128)(2,1)}, bf16[384,256]{1,0:T(8,128)(2,1)S(1)}, u32[]{:S(2)}) copy-start(bf16[384,256]{1,0:T(8,128)(2,1)S(1)} %collective-permute-done.p1) | copy-start | bytes 589828
  33.9 8.0 %collective-permute-start.2 = (bf16[384,256]{1,0:T(8,128)(2,1)S(1)}, bf16[384,256]{1,0:T(8,128)(2,1)S(1)}, u32[]{:S(2)}, u32[]{:S(2)}) collective-permute-start(bf16[384,256]{1,0:T(8,128)(2,1)S(1)} %get-tuple-element.67), channel_id=1, source_target_pairs={{0,3},{1,2},{2,1},{3,0},{4,7},{5,6},{6,5},{7,4},{8,11},{9,10},{10,... | collective-permute-start | bytes 589832 | tf_op jit(solution)/shard_map/ppermute | solution.py:913
  35.5 37.0 %copy-start.6 = (bf16[384,256]{1,0:T(8,128)(2,1)}, bf16[384,256]{1,0:T(8,128)(2,1)S(1)}, u32[]{:S(2)}) copy-start(bf16[384,256]{1,0:T(8,128)(2,1)S(1)} %collective-permute-done.1.p2) | copy-start | bytes 589828
  35.5 36.9 %collective-permute-start.12 = (bf16[576,384]{1,0:T(8,128)(2,1)S(1)}, bf16[576,384]{1,0:T(8,128)(2,1)}, u32[]{:S(2)}, u32[]{:S(2)}) collective-permute-start(bf16[576,384]{1,0:T(8,128)(2,1)S(1)} %join.1.refs_0_), channel_id=1, source_target_pairs={{0,4},{4,0},{8,12},{12,8},{16,20},{20,16},{24,28},{28,24},{1,5},{5... | collective-permute-start | bytes 1327112 | tf_op jit(solution)/shard_map/ppermute | solution.py:913
  35.5 37.0 %copy-start.24 = (bf16[576,384]{1,0:T(8,128)(2,1)}, bf16[576,384]{1,0:T(8,128)(2,1)S(1)}, u32[]{:S(2)}) copy-start(bf16[576,384]{1,0:T(8,128)(2,1)S(1)} %collective-permute-done.11.refs_3_) | copy-start | bytes 1327108
  35.5 36.9 %collective-permute-start.15 = (bf16[576,384]{1,0:T(8,128)(2,1)S(1)}, bf16[576,384]{1,0:T(8,128)(2,1)}, u32[]{:S(2)}, u32[]{:S(2)}) collective-permute-start(bf16[576,384]{1,0:T(8,128)(2,1)S(1)} %collective-permute-done.11.refs_3_), channel_id=1, source_target_pairs={{0,4},{4,0},{8,12},{12,8},{16,20},{20,16},{24,28},{28,24},{1,5},{5... | collective-permute-start | bytes 1327112 | tf_op jit(solution)/shard_map/ppermute | solution.py:913
  41.2 31.3 %copy-start.25 = (bf16[576,384]{1,0:T(8,128)(2,1)}, bf16[576,384]{1,0:T(8,128)(2,1)S(1)}, u32[]{:S(2)}) copy-start(bf16[576,384]{1,0:T(8,128)(2,1)S(1)} %collective-permute-done.10.refs_2_) | copy-start | bytes 1327108
  41.2 31.2 %collective-permute-start.14 = (bf16[576,384]{1,0:T(8,128)(2,1)S(1)}, bf16[576,384]{1,0:T(8,128)(2,1)}, u32[]{:S(2)}, u32[]{:S(2)}) collective-permute-start(bf16[576,384]{1,0:T(8,128)(2,1)S(1)} %collective-permute-done.10.refs_2_), channel_id=1, source_target_pairs={{0,4},{4,0},{8,12},{12,8},{16,20},{20,16},{24,28},{28,24},{1,5},{5... | collective-permute-start | bytes 1327112 | tf_op jit(solution)/shard_map/ppermute | solution.py:913
  41.3 31.2 %copy-start.26 = (bf16[576,384]{1,0:T(8,128)(2,1)}, bf16[576,384]{1,0:T(8,128)(2,1)S(1)}, u32[]{:S(2)}) copy-start(bf16[576,384]{1,0:T(8,128)(2,1)S(1)} %collective-permute-done.9.refs_1_) | copy-start | bytes 1327108
  41.3 31.1 %collective-permute-start.13 = (bf16[576,384]{1,0:T(8,128)(2,1)S(1)}, bf16[576,384]{1,0:T(8,128)(2,1)}, u32[]{:S(2)}, u32[]{:S(2)}) collective-permute-start(bf16[576,384]{1,0:T(8,128)(2,1)S(1)} %collective-permute-done.9.refs_1_), channel_id=1, source_target_pairs={{0,4},{4,0},{8,12},{12,8},{16,20},{20,16},{24,28},{28,24},{1,5},{5... | collective-permute-start | bytes 1327112 | tf_op jit(solution)/shard_map/ppermute | solution.py:913
  41.9 30.6 %copy-start.8 = (bf16[384,256]{1,0:T(8,128)(2,1)}, bf16[384,256]{1,0:T(8,128)(2,1)S(1)}, u32[]{:S(2)}) copy-start(bf16[384,256]{1,0:T(8,128)(2,1)S(1)} %collective-permute-done.2.p3) | copy-start | bytes 589828
  55.5 4.8 %collective-permute-start.3 = (bf16[192,256]{1,0:T(8,128)(2,1)S(1)}, bf16[192,256]{1,0:T(8,128)(2,1)S(1)}, u32[]{:S(2)}, u32[]{:S(2)}) collective-permute-start(bf16[192,256]{1,0:T(8,128)(2,1)S(1)} %get-tuple-element.69.o1), channel_id=1, source_target_pairs={{0,1},{1,0},{2,3},{3,2},{4,5},{5,4},{6,7},{7,6},{8,9},{9,8},{10,11... | collective-permute-start | bytes 294920 | tf_op jit(solution)/shard_map/ppermute | solution.py:913
  60.3 5.6 %collective-permute-start.4 = (bf16[192,256]{1,0:T(8,128)(2,1)S(1)}, bf16[192,256]{1,0:T(8,128)(2,1)S(1)}, u32[]{:S(2)}, u32[]{:S(2)}) collective-permute-start(bf16[192,256]{1,0:T(8,128)(2,1)S(1)} %get-tuple-element.70.o2), channel_id=1, source_target_pairs={{0,2},{1,3},{2,0},{3,1},{4,6},{5,7},{6,4},{7,5},{8,10},{9,11},{10,... | collective-permute-start | bytes 294920 | tf_op jit(solution)/shard_map/ppermute | solution.py:913
  65.9 6.5 %collective-permute-start.5 = (bf16[192,256]{1,0:T(8,128)(2,1)S(1)}, bf16[192,256]{1,0:T(8,128)(2,1)S(1)}, u32[]{:S(2)}, u32[]{:S(2)}) collective-permute-start(bf16[192,256]{1,0:T(8,128)(2,1)S(1)} %get-tuple-element.71.o3), channel_id=1, source_target_pairs={{0,3},{1,2},{2,1},{3,0},{4,7},{5,6},{6,5},{7,4},{8,11},{9,10},{10,... | collective-permute-start | bytes 294920 | tf_op jit(solution)/shard_map/ppermute | solution.py:913
  84.9 4.0 %collective-permute-start.34 = (bf16[2368,384]{1,0:T(8,128)(2,1)}, bf16[2368,384]{1,0:T(8,128)(2,1)S(1)}, u32[]{:S(2)}, u32[]{:S(2)}) collective-permute-start(bf16[2368,384]{1,0:T(8,128)(2,1)} %get-tuple-element.98), channel_id=1, source_target_pairs={{0,4},{4,0},{8,12},{12,8},{16,20},{20,16},{24,28},{28,24},{1,5},{5... | collective-permute-start | bytes 5455880 | tf_op jit(solution)/shard_map/ppermute | solution.py:913
  92.1 30.0 %collective-permute-start.35 = (bf16[640,384]{1,0:T(8,128)(2,1)S(1)}, bf16[640,384]{1,0:T(8,128)(2,1)S(1)}, u32[]{:S(2)}, u32[]{:S(2)}) collective-permute-start(bf16[640,384]{1,0:T(8,128)(2,1)S(1)} %get-tuple-element.100), channel_id=1, source_target_pairs={{0,8},{4,12},{8,0},{12,4},{16,24},{20,28},{24,16},{28,20},{1,9},{5... | collective-permute-start | bytes 1474568 | tf_op jit(solution)/shard_map/ppermute | solution.py:913
  93.7 28.4 %collective-permute-start.36 = (bf16[640,384]{1,0:T(8,128)(2,1)S(1)}, bf16[640,384]{1,0:T(8,128)(2,1)S(1)}, u32[]{:S(2)}, u32[]{:S(2)}) collective-permute-start(bf16[640,384]{1,0:T(8,128)(2,1)S(1)} %get-tuple-element.101), channel_id=1, source_target_pairs={{0,16},{4,20},{8,24},{12,28},{16,0},{20,4},{24,8},{28,12},{1,17},{... | collective-permute-start | bytes 1474568 | tf_op jit(solution)/shard_map/ppermute | solution.py:913
  95.1 27.1 %collective-permute-start.37 = (bf16[640,384]{1,0:T(8,128)(2,1)S(1)}, bf16[640,384]{1,0:T(8,128)(2,1)S(1)}, u32[]{:S(2)}, u32[]{:S(2)}) collective-permute-start(bf16[640,384]{1,0:T(8,128)(2,1)S(1)} %get-tuple-element.102), channel_id=1, source_target_pairs={{0,24},{4,28},{8,16},{12,20},{16,8},{20,12},{24,0},{28,4},{1,25},{... | collective-permute-start | bytes 1474568 | tf_op jit(solution)/shard_map/ppermute | solution.py:913
  95.7 5.6 %collective-permute-start.16 = (bf16[192,256]{1,0:T(8,128)(2,1)S(1)}, bf16[192,256]{1,0:T(8,128)(2,1)S(1)}, u32[]{:S(2)}, u32[]{:S(2)}) collective-permute-start(bf16[192,256]{1,0:T(8,128)(2,1)S(1)} %copy-done.34), channel_id=1, source_target_pairs={{0,1},{1,0},{2,3},{3,2},{4,5},{5,4},{6,7},{7,6},{8,9},{9,8},{10,11... | collective-permute-start | bytes 294920 | tf_op jit(solution)/shard_map/ppermute | solution.py:913
  96.8 8.4 %collective-permute-start.17 = (bf16[192,256]{1,0:T(8,128)(2,1)S(1)}, bf16[192,256]{1,0:T(8,128)(2,1)S(1)}, u32[]{:S(2)}, u32[]{:S(2)}) collective-permute-start(bf16[192,256]{1,0:T(8,128)(2,1)S(1)} %copy-done.33), channel_id=1, source_target_pairs={{0,2},{1,3},{2,0},{3,1},{4,6},{5,7},{6,4},{7,5},{8,10},{9,11},{10,... | collective-permute-start | bytes 294920 | tf_op jit(solution)/shard_map/ppermute | solution.py:913
  101.3 6.4 %collective-permute-start.18 = (bf16[192,256]{1,0:T(8,128)(2,1)S(1)}, bf16[192,256]{1,0:T(8,128)(2,1)S(1)}, u32[]{:S(2)}, u32[]{:S(2)}) collective-permute-start(bf16[192,256]{1,0:T(8,128)(2,1)S(1)} %copy-done.32), channel_id=1, source_target_pairs={{0,3},{1,2},{2,1},{3,0},{4,7},{5,6},{6,5},{7,4},{8,11},{9,10},{10,... | collective-permute-start | bytes 294920 | tf_op jit(solution)/shard_map/ppermute | solution.py:913
  119.3 9.3 %collective-permute-start.22 = (bf16[144,192]{1,0:T(8,128)(2,1)S(1)}, bf16[144,192]{1,0:T(8,128)(2,1)S(1)}, u32[]{:S(2)}, u32[]{:S(2)}) collective-permute-start(bf16[144,192]{1,0:T(8,128)(2,1)S(1)} %get-tuple-element.89), channel_id=1, source_target_pairs={{0,1},{1,0},{2,3},{3,2},{4,5},{5,4},{6,7},{7,6},{8,9},{9,8},{10,11... | collective-permute-start | bytes 165896 | tf_op jit(solution)/shard_map/ppermute | solution.py:913
  119.3 9.3 %collective-permute-start.23 = (bf16[144,192]{1,0:T(8,128)(2,1)S(1)}, bf16[144,192]{1,0:T(8,128)(2,1)S(1)}, u32[]{:S(2)}, u32[]{:S(2)}) collective-permute-start(bf16[144,192]{1,0:T(8,128)(2,1)S(1)} %get-tuple-element.90), channel_id=1, source_target_pairs={{0,2},{1,3},{2,0},{3,1},{4,6},{5,7},{6,4},{7,5},{8,10},{9,11},{10,... | collective-permute-start | bytes 165896 | tf_op jit(solution)/shard_map/ppermute | solution.py:913
  122.1 37.3 %copy-start.11 = (f32[256,768]{1,0:T(8,128)S(1)}, f32[256,768]{1,0:T(8,128)}, u32[]{:S(2)}) copy-start(f32[256,768]{1,0:T(8,128)} %get-tuple-element.73.d_resid) | copy-start | bytes 2359300
  122.9 16.5 %collective-permute-start.38 = (bf16[208,384]{1,0:T(8,128)(2,1)S(1)}, bf16[208,384]{1,0:T(8,128)(2,1)S(1)}, u32[]{:S(2)}, u32[]{:S(2)}) collective-permute-start(bf16[208,384]{1,0:T(8,128)(2,1)S(1)} %get-tuple-element.104), channel_id=1, source_target_pairs={{0,1},{1,0},{2,3},{3,2},{4,5},{5,4},{6,7},{7,6},{8,9},{9,8},{10,11... | collective-permute-start | bytes 479240 | tf_op jit(solution)/shard_map/ppermute | solution.py:913
  123.6 16.2 %collective-permute-start.39 = (bf16[208,384]{1,0:T(8,128)(2,1)S(1)}, bf16[208,384]{1,0:T(8,128)(2,1)S(1)}, u32[]{:S(2)}, u32[]{:S(2)}) collective-permute-start(bf16[208,384]{1,0:T(8,128)(2,1)S(1)} %get-tuple-element.105), channel_id=1, source_target_pairs={{0,2},{1,3},{2,0},{3,1},{4,6},{5,7},{6,4},{7,5},{8,10},{9,11},{10,... | collective-permute-start | bytes 479240 | tf_op jit(solution)/shard_map/ppermute | solution.py:913
  125.1 1.2 collective-permute-start.29
  126.3 7.1 %collective-permute-start.24 = (bf16[144,192]{1,0:T(8,128)(2,1)S(1)}, bf16[144,192]{1,0:T(8,128)(2,1)S(1)}, u32[]{:S(2)}, u32[]{:S(2)}) collective-permute-start(bf16[144,192]{1,0:T(8,128)(2,1)S(1)} %get-tuple-element.91), channel_id=1, source_target_pairs={{0,3},{1,2},{2,1},{3,0},{4,7},{5,6},{6,5},{7,4},{8,11},{9,10},{10,... | collective-permute-start | bytes 165896 | tf_op jit(solution)/shard_map/ppermute | solution.py:913
  128.6 4.9 %collective-permute-start.25 = (bf16[144,192]{1,0:T(8,128)(2,1)S(1)}, bf16[144,192]{1,0:T(8,128)(2,1)S(1)}, u32[]{:S(2)}, u32[]{:S(2)}) collective-permute-start(bf16[144,192]{1,0:T(8,128)(2,1)S(1)} %get-tuple-element.88.w0), channel_id=1, source_target_pairs={{0,4},{4,0},{8,12},{12,8},{16,20},{20,16},{24,28},{28,24},{1,5},{5... | collective-permute-start | bytes 165896 | tf_op jit(solution)/shard_map/ppermute | solution.py:913
  128.6 5.4 %collective-permute-start.26 = (bf16[144,192]{1,0:T(8,128)(2,1)S(1)}, bf16[144,192]{1,0:T(8,128)(2,1)S(1)}, u32[]{:S(2)}, u32[]{:S(2)}) collective-permute-start(bf16[144,192]{1,0:T(8,128)(2,1)S(1)} %collective-permute-done.22.w1), channel_id=1, source_target_pairs={{0,4},{4,0},{8,12},{12,8},{16,20},{20,16},{24,28},{28,24},{1,5},{5... | collective-permute-start | bytes 165896 | tf_op jit(solution)/shard_map/ppermute | solution.py:913
  133.5 2.1 %collective-permute-start.27 = (bf16[144,192]{1,0:T(8,128)(2,1)S(1)}, bf16[144,192]{1,0:T(8,128)(2,1)S(1)}, u32[]{:S(2)}, u32[]{:S(2)}) collective-permute-start(bf16[144,192]{1,0:T(8,128)(2,1)S(1)} %collective-permute-done.23.w2), channel_id=1, source_target_pairs={{0,4},{4,0},{8,12},{12,8},{16,20},{20,16},{24,28},{28,24},{1,5},{5... | collective-permute-start | bytes 165896 | tf_op jit(solution)/shard_map/ppermute | solution.py:913
  133.5 2.1 %collective-permute-start.28 = (bf16[144,192]{1,0:T(8,128)(2,1)S(1)}, bf16[144,192]{1,0:T(8,128)(2,1)S(1)}, u32[]{:S(2)}, u32[]{:S(2)}) collective-permute-start(bf16[144,192]{1,0:T(8,128)(2,1)S(1)} %collective-permute-done.24.w3), channel_id=1, source_target_pairs={{0,4},{4,0},{8,12},{12,8},{16,20},{20,16},{24,28},{28,24},{1,5},{5... | collective-permute-start | bytes 165896 | tf_op jit(solution)/shard_map/ppermute | solution.py:913
  134.0 8.1 %collective-permute-start.40 = (bf16[208,384]{1,0:T(8,128)(2,1)S(1)}, bf16[208,384]{1,0:T(8,128)(2,1)S(1)}, u32[]{:S(2)}, u32[]{:S(2)}) collective-permute-start(bf16[208,384]{1,0:T(8,128)(2,1)S(1)} %get-tuple-element.106), channel_id=1, source_target_pairs={{0,3},{1,2},{2,1},{3,0},{4,7},{5,6},{6,5},{7,4},{8,11},{9,10},{10,... | collective-permute-start | bytes 479240 | tf_op jit(solution)/shard_map/ppermute | solution.py:913
  136.2 10.1 %collective-permute-start.32 = (bf16[320,192]{1,0:T(8,128)(2,1)S(1)}, bf16[320,192]{1,0:T(8,128)(2,1)S(1)}, u32[]{:S(2)}, u32[]{:S(2)}) collective-permute-start(bf16[320,192]{1,0:T(8,128)(2,1)S(1)} %qkv_core.1.m0), channel_id=1, source_target_pairs={{0,24},{4,28},{8,16},{12,20},{16,8},{20,12},{24,0},{28,4},{1,25},{... | collective-permute-start | bytes 368648 | tf_op jit(solution)/shard_map/ppermute | solution.py:913
  139.0 9.2 %collective-permute-start.31 = (bf16[320,192]{1,0:T(8,128)(2,1)S(1)}, bf16[320,192]{1,0:T(8,128)(2,1)S(1)}, u32[]{:S(2)}, u32[]{:S(2)}) collective-permute-start(bf16[320,192]{1,0:T(8,128)(2,1)S(1)} %qkv_core.1.m0), channel_id=1, source_target_pairs={{0,16},{4,20},{8,24},{12,28},{16,0},{20,4},{24,8},{28,12},{1,17},{... | collective-permute-start | bytes 368648 | tf_op jit(solution)/shard_map/ppermute | solution.py:913
  139.4 10.9 %collective-permute-start.30 = (bf16[320,192]{1,0:T(8,128)(2,1)S(1)}, bf16[320,192]{1,0:T(8,128)(2,1)S(1)}, u32[]{:S(2)}, u32[]{:S(2)}) collective-permute-start(bf16[320,192]{1,0:T(8,128)(2,1)S(1)} %qkv_core.1.m0), channel_id=1, source_target_pairs={{0,8},{4,12},{8,0},{12,4},{16,24},{20,28},{24,16},{28,20},{1,9},{5... | collective-permute-start | bytes 368648 | tf_op jit(solution)/shard_map/ppermute | solution.py:913
  139.8 5.6 %collective-permute-start.19 = (bf16[192,256]{1,0:T(8,128)(2,1)S(1)}, bf16[192,256]{1,0:T(8,128)(2,1)S(1)}, u32[]{:S(2)}, u32[]{:S(2)}) collective-permute-start(bf16[192,256]{1,0:T(8,128)(2,1)S(1)} %get-tuple-element.85), channel_id=1, source_target_pairs={{0,1},{1,0},{2,3},{3,2},{4,5},{5,4},{6,7},{7,6},{8,9},{9,8},{10,11... | collective-permute-start | bytes 294920 | tf_op jit(solution)/shard_map/ppermute | solution.py:913
  142.7 16.1 %collective-permute-start.43 = (bf16[144,384]{1,0:T(8,128)(2,1)S(1)}, bf16[144,384]{1,0:T(8,128)(2,1)S(1)}, u32[]{:S(2)}, u32[]{:S(2)}) collective-permute-start(bf16[144,384]{1,0:T(8,128)(2,1)S(1)} %get-tuple-element.108.n0), channel_id=1, source_target_pairs={{0,24},{4,28},{8,16},{12,20},{16,8},{20,12},{24,0},{28,4},{1,25},{... | collective-permute-start | bytes 331784 | tf_op jit(solution)/shard_map/ppermute | solution.py:913
  145.3 13.6 %collective-permute-start.42 = (bf16[144,384]{1,0:T(8,128)(2,1)S(1)}, bf16[144,384]{1,0:T(8,128)(2,1)S(1)}, u32[]{:S(2)}, u32[]{:S(2)}) collective-permute-start(bf16[144,384]{1,0:T(8,128)(2,1)S(1)} %get-tuple-element.108.n0), channel_id=1, source_target_pairs={{0,16},{4,20},{8,24},{12,28},{16,0},{20,4},{24,8},{28,12},{1,17},{... | collective-permute-start | bytes 331784 | tf_op jit(solution)/shard_map/ppermute | solution.py:913
  146.3 13.1 %collective-permute-start.41 = (bf16[144,384]{1,0:T(8,128)(2,1)S(1)}, bf16[144,384]{1,0:T(8,128)(2,1)S(1)}, u32[]{:S(2)}, u32[]{:S(2)}) collective-permute-start(bf16[144,384]{1,0:T(8,128)(2,1)S(1)} %get-tuple-element.108.n0), channel_id=1, source_target_pairs={{0,8},{4,12},{8,0},{12,4},{16,24},{20,28},{24,16},{28,20},{1,9},{5... | collective-permute-start | bytes 331784 | tf_op jit(solution)/shard_map/ppermute | solution.py:913
  148.2 10.1 %collective-permute-start.20 = (bf16[192,256]{1,0:T(8,128)(2,1)S(1)}, bf16[192,256]{1,0:T(8,128)(2,1)S(1)}, u32[]{:S(2)}, u32[]{:S(2)}) collective-permute-start(bf16[192,256]{1,0:T(8,128)(2,1)S(1)} %get-tuple-element.86), channel_id=1, source_target_pairs={{0,2},{1,3},{2,0},{3,1},{4,6},{5,7},{6,4},{7,5},{8,10},{9,11},{10,... | collective-permute-start | bytes 294920 | tf_op jit(solution)/shard_map/ppermute | solution.py:913
  150.3 8.1 %collective-permute-start.21 = (bf16[192,256]{1,0:T(8,128)(2,1)S(1)}, bf16[192,256]{1,0:T(8,128)(2,1)S(1)}, u32[]{:S(2)}, u32[]{:S(2)}) collective-permute-start(bf16[192,256]{1,0:T(8,128)(2,1)S(1)} %get-tuple-element.87), channel_id=1, source_target_pairs={{0,3},{1,2},{2,1},{3,0},{4,7},{5,6},{6,5},{7,4},{8,11},{9,10},{10,... | collective-permute-start | bytes 294920 | tf_op jit(solution)/shard_map/ppermute | solution.py:913
  158.4 2.7 %collective-permute-start.33 = (bf16[288,192]{1,0:T(8,128)(2,1)S(1)}, bf16[288,192]{1,0:T(8,128)(2,1)S(1)}, u32[]{:S(2)}, u32[]{:S(2)}) collective-permute-start(bf16[288,192]{1,0:T(8,128)(2,1)S(1)} %get-tuple-element.93.near), channel_id=1, source_target_pairs={{0,4},{4,0},{8,12},{12,8},{16,20},{20,16},{24,28},{28,24},{1,5},{5... | collective-permute-start | bytes 331784 | tf_op jit(solution)/shard_map/ppermute | solution.py:913
  158.4 4.1 %collective-permute-start.44 = (bf16[144,384]{1,0:T(8,128)(2,1)S(1)}, bf16[144,384]{1,0:T(8,128)(2,1)S(1)}, u32[]{:S(2)}, u32[]{:S(2)}) collective-permute-start(bf16[144,384]{1,0:T(8,128)(2,1)S(1)} %get-tuple-element.108.n0), channel_id=1, source_target_pairs={{0,4},{4,0},{8,12},{12,8},{16,20},{20,16},{24,28},{28,24},{1,5},{5... | collective-permute-start | bytes 331784 | tf_op jit(solution)/shard_map/ppermute | solution.py:913
  158.9 3.6 %collective-permute-start.47 = (bf16[144,384]{1,0:T(8,128)(2,1)S(1)}, bf16[144,384]{1,0:T(8,128)(2,1)S(1)}, u32[]{:S(2)}, u32[]{:S(2)}) collective-permute-start(bf16[144,384]{1,0:T(8,128)(2,1)S(1)} %collective-permute-done.43.n3), channel_id=1, source_target_pairs={{0,4},{4,0},{8,12},{12,8},{16,20},{20,16},{24,28},{28,24},{1,5},{5... | collective-permute-start | bytes 331784 | tf_op jit(solution)/shard_map/ppermute | solution.py:913
  159.0 3.6 %collective-permute-start.46 = (bf16[144,384]{1,0:T(8,128)(2,1)S(1)}, bf16[144,384]{1,0:T(8,128)(2,1)S(1)}, u32[]{:S(2)}, u32[]{:S(2)}) collective-permute-start(bf16[144,384]{1,0:T(8,128)(2,1)S(1)} %collective-permute-done.42.n2), channel_id=1, source_target_pairs={{0,4},{4,0},{8,12},{12,8},{16,20},{20,16},{24,28},{28,24},{1,5},{5... | collective-permute-start | bytes 331784 | tf_op jit(solution)/shard_map/ppermute | solution.py:913
  159.4 3.1 %collective-permute-start.45 = (bf16[144,384]{1,0:T(8,128)(2,1)S(1)}, bf16[144,384]{1,0:T(8,128)(2,1)S(1)}, u32[]{:S(2)}, u32[]{:S(2)}) collective-permute-start(bf16[144,384]{1,0:T(8,128)(2,1)S(1)} %collective-permute-done.41.n1), channel_id=1, source_target_pairs={{0,4},{4,0},{8,12},{12,8},{16,20},{20,16},{24,28},{28,24},{1,5},{5... | collective-permute-start | bytes 331784 | tf_op jit(solution)/shard_map/ppermute | solution.py:913
  (25 other events, 278.9 us)
